TPU v7x, 256 devices: a whole 4x4x8 slice. The times are simulated.
256 devices in a mesh: row: 4 (over y_lo, core), col: 64 (over x, y_hi, z).
Axes of the slice: x: 4, y: 4 (y_hi: 2, y_lo: 2; y = y_hi * 2 + y_lo), z: 8, core: 2. Of those that a mesh axis runs over, the one named last changes fastest.
Arguments:
- tensor: bfloat16 [128, 3072, 4096], P(None, 'col', 'row'), may hold values from -6 to 6
- first_factor: bfloat16 [64, 4096], P(None, ('row', 'col')), may hold values from -0.453125 to 0.453125
- second_factor: bfloat16 [64, 3072], P(None, 'col'), may hold values from -0.5232237 to 0.5232237
Outputs:
- frames: float32 [64, 128], replicated
- mode_one: float32 [64, 4096], P(None, ('row', 'col'))
All inputs are finite; a program needn't handle non-finite values.
Results may differ from a plain program's by a relative error of at most 0.004.
Values may be sent and summed in bfloat16 or wider, within the bound.
A program may use at most 128 MiB of HBM per device.

v0:
```python
import functools

import jax
import jax.numpy as jnp
from jax import lax
from jax.experimental import pallas as pl
from jax.experimental.pallas import tpu as pltpu
from jax.sharding import PartitionSpec as P

ridge_weight = 0.05
MESH_ID = pl.DeviceIdType.MESH


def ridge_solve(gram, right_side):
    order_size = gram.shape[0]
    factor_low = jnp.linalg.cholesky(gram + ridge_weight * jnp.eye(order_size, dtype=jnp.float32))
    middle = lax.linalg.triangular_solve(factor_low, right_side, left_side=True, lower=True)
    return lax.linalg.triangular_solve(
        factor_low, middle, left_side=True, lower=True, transpose_a=True
    )


def gram_of(factor):
    return jnp.dot(factor, factor.T, preferred_element_type=jnp.float32)


STREAM_FRAMES = 16


def _frame_kernel(block_t_ref, second_t_ref, slab_ref, out_ref):
    frames, width, rows = slab_ref.shape
    projected = jnp.dot(
        slab_ref[...].reshape(frames * width, rows), block_t_ref[...],
        preferred_element_type=jnp.float32,
    ).reshape(frames, width, block_t_ref.shape[1])
    out_ref[...] = jnp.sum(projected * second_t_ref[...][None], axis=1)


def _second_kernel(block_t_ref, frames_t_ref, slab_ref, out_ref):
    frames, width, rows = slab_ref.shape

    @pl.when(pl.program_id(0) == 0)
    def _():
        out_ref[...] = jnp.zeros_like(out_ref)

    projected = jnp.dot(
        slab_ref[...].reshape(frames * width, rows), block_t_ref[...],
        preferred_element_type=jnp.float32,
    ).reshape(frames, width, block_t_ref.shape[1])
    out_ref[...] += jnp.sum(projected * frames_t_ref[...][:, None, :], axis=0)


def _slab_spec(width, rows):
    return pl.BlockSpec((STREAM_FRAMES, width, rows), lambda s: (s, 0, 0))


def _whole(shape):
    return pl.BlockSpec(shape, lambda s: (0,) * len(shape))


def frame_pass(tensor, block_t, second_t):
    frame_count, width, rows = tensor.shape
    components = block_t.shape[1]
    return pl.pallas_call(
        _frame_kernel,
        grid=(frame_count // STREAM_FRAMES,),
        in_specs=[_whole(block_t.shape), _whole(second_t.shape), _slab_spec(width, rows)],
        out_specs=pl.BlockSpec((STREAM_FRAMES, components), lambda s: (s, 0)),
        out_shape=jax.ShapeDtypeStruct((frame_count, components), jnp.float32),
        cost_estimate=pl.CostEstimate(
            flops=2 * components * frame_count * width * rows, transcendentals=0,
            bytes_accessed=2 * frame_count * width * rows,
        ),
    )(block_t, second_t, tensor)


def second_pass(tensor, block_t, frames_t):
    frame_count, width, rows = tensor.shape
    components = block_t.shape[1]
    return pl.pallas_call(
        _second_kernel,
        grid=(frame_count // STREAM_FRAMES,),
        in_specs=[
            _whole(block_t.shape),
            pl.BlockSpec((STREAM_FRAMES, components), lambda s: (s, 0)),
            _slab_spec(width, rows),
        ],
        out_specs=_whole((width, components)),
        out_shape=jax.ShapeDtypeStruct((width, components), jnp.float32),
        cost_estimate=pl.CostEstimate(
            flops=2 * components * frame_count * width * rows, transcendentals=0,
            bytes_accessed=2 * frame_count * width * rows,
        ),
    )(block_t, frames_t, tensor)


def _accumulate_kernel(frames_ref, tiled_ref, slab_ref, out_ref):
    frames, width, rows = slab_ref.shape
    step = pl.program_id(0)

    @pl.when(step == 0)
    def _():
        out_ref[...] = jnp.zeros_like(out_ref)

    frame_count = frames_ref.shape[1]
    span = frames * width
    which = lax.broadcasted_iota(jnp.int32, (frame_count, span), 0) - step * frames
    column = lax.broadcasted_iota(jnp.int32, (frame_count, span), 1)
    expand = ((column >= which * width) & (column < which * width + width)).astype(jnp.bfloat16)
    rest = frames_ref[...]
    repeated = jnp.zeros((frames_ref.shape[0], span), jnp.float32)
    for _ in range(3):
        piece = rest.astype(jnp.bfloat16)
        rest = rest - piece.astype(jnp.float32)
        repeated = repeated + jnp.dot(piece, expand, preferred_element_type=jnp.float32)
    weights = (repeated * tiled_ref[...]).astype(jnp.bfloat16)
    out_ref[...] += jnp.dot(
        weights, slab_ref[...].reshape(span, rows), preferred_element_type=jnp.float32
    )


def accumulate_pass(tensor, frames, second):
    frame_count, width, rows = tensor.shape
    components = frames.shape[0]
    tiled = jnp.tile(second, (1, STREAM_FRAMES))
    return pl.pallas_call(
        _accumulate_kernel,
        grid=(frame_count // STREAM_FRAMES,),
        in_specs=[_whole(frames.shape), _whole(tiled.shape), _slab_spec(width, rows)],
        out_specs=_whole((components, rows)),
        out_shape=jax.ShapeDtypeStruct((components, rows), jnp.float32),
        cost_estimate=pl.CostEstimate(
            flops=2 * components * frame_count * width * rows, transcendentals=0,
            bytes_accessed=2 * frame_count * width * rows,
        ),
    )(frames, tiled, tensor)


def _exchange_kernel(n, mode, send_ref, out_ref, recv, send_sems, recv_sems, *extra):
    me = lax.axis_index("col")
    row = lax.axis_index("row")
    broadcast = mode == "gather"

    def exchange(source, landing, sends, recvs):
        def descriptor(peer, slot):
            return pltpu.make_async_remote_copy(
                src_ref=source(peer),
                dst_ref=landing.at[slot],
                send_sem=sends.at[peer],
                recv_sem=recvs.at[slot],
                device_id=(row, peer),
                device_id_type=MESH_ID,
            )

        def start(t, carry):
            peer = lax.rem(me + 1 + t, n)
            descriptor(peer, me).start()
            return carry

        lax.fori_loop(0, n - 1, start, 0)

        def finish(t, carry):
            peer = lax.rem(me + 1 + t, n)
            copy = descriptor(peer, peer)
            copy.wait_send()
            copy.wait_recv()
            return carry

        lax.fori_loop(0, n - 1, finish, 0)
        landing[me] = source(me)[...]

    barrier = pltpu.get_barrier_semaphore()

    def greet(t, carry):
        peer = lax.rem(me + 1 + t, n)
        pl.semaphore_signal(barrier, inc=1, device_id=(row, peer), device_id_type=MESH_ID)
        return carry

    lax.fori_loop(0, n - 1, greet, 0)
    pl.semaphore_wait(barrier, n - 1)
    exchange((lambda peer: send_ref) if broadcast else (lambda peer: send_ref.at[peer]), recv, send_sems, recv_sems)
    if mode == "gather":
        out_ref[...] = recv[...]
    elif mode == "scatter":
        out_ref[...] = jnp.sum(recv[...], axis=0)
    else:
        chunk, recv_back, back_send_sems, back_recv_sems = extra
        chunk[...] = jnp.sum(recv[...], axis=0)
        exchange(lambda peer: chunk, recv_back, back_send_sems, back_recv_sems)
        out_ref[...] = recv_back[...]


def col_exchange(send, n, mode, collective_id):
    piece = tuple(send.shape) if mode == "gather" else tuple(send.shape[1:])
    out_shape = piece if mode == "scatter" else (n,) + piece
    scratch = [
        pltpu.VMEM((n,) + piece, send.dtype),
        pltpu.SemaphoreType.DMA((n,)),
        pltpu.SemaphoreType.DMA((n,)),
    ]
    if mode == "allreduce":
        scratch += [
            pltpu.VMEM(piece, send.dtype),
            pltpu.VMEM((n,) + piece, send.dtype),
            pltpu.SemaphoreType.DMA((n,)),
            pltpu.SemaphoreType.DMA((n,)),
        ]
    return pl.pallas_call(
        functools.partial(_exchange_kernel, n, mode),
        out_shape=jax.ShapeDtypeStruct(out_shape, send.dtype),
        in_specs=[pl.BlockSpec(memory_space=pltpu.VMEM)],
        out_specs=pl.BlockSpec(memory_space=pltpu.VMEM),
        scratch_shapes=scratch,
        compiler_params=pltpu.CompilerParams(collective_id=collective_id, has_side_effects=True),
    )(send)


def col_gather_t(piece_t, n):
    gathered = col_exchange(piece_t, n, "gather", 0)
    return gathered.reshape(n * piece_t.shape[0], piece_t.shape[1])


def col_reduce_scatter(full, n, collective_id):
    width = full.shape[1] // n
    summed_t = col_exchange(full.T.reshape(n, width, full.shape[0]), n, "scatter", collective_id)
    return summed_t.T


def col_all_reduce(full, n, collective_id):
    width = full.shape[1] // n
    summed_t = col_exchange(full.T.reshape(n, width, full.shape[0]), n, "allreduce", collective_id)
    return summed_t.reshape(n * width, full.shape[0]).T


def local(tensor, first_factor, second_factor):
    frame_count, col_count, row_count = tensor.shape
    components = first_factor.shape[0]
    n = lax.axis_size("col")
    second_values = second_factor.astype(jnp.float32)
    gram_first_part = gram_of(first_factor)
    gram_second_part = gram_of(second_factor)
    block_t = col_gather_t(first_factor.T, n)
    frame_part = frame_pass(tensor, block_t, second_values.T).T
    row_summed = lax.psum(jnp.concatenate([frame_part, gram_first_part], axis=1), "row")
    summed = col_all_reduce(jnp.concatenate([row_summed, gram_second_part], axis=1), n, 3)
    frame_sum = summed[:, :frame_count]
    gram_first = summed[:, frame_count:frame_count + components]
    gram_second = summed[:, frame_count + components:]
    frames = ridge_solve(gram_first * gram_second, frame_sum)
    gram_frames = jnp.dot(frames, frames.T, precision=lax.Precision.HIGHEST)
    full_part = accumulate_pass(tensor, frames, second_values)
    first_sum_mine = col_reduce_scatter(full_part, n, 1)
    new_first_mine = ridge_solve(gram_second * gram_frames, first_sum_mine).astype(jnp.bfloat16)
    new_block_t = col_gather_t(new_first_mine.T, n)
    gram_new_part = lax.dot_general(
        new_block_t, new_block_t, (((0,), (0,)), ((), ())), preferred_element_type=jnp.float32
    )
    second_part = second_pass(tensor, new_block_t, frames.T).T
    second_sum, gram_new = lax.psum((second_part, gram_new_part), "row")
    new_second = ridge_solve(gram_new * gram_frames, second_sum)
    full_next = accumulate_pass(tensor, frames, new_second)
    mode_one = col_reduce_scatter(full_next, n, 2)
    return (frames, mode_one)


def solution(mesh):
    return jax.shard_map(
        local,
        mesh=mesh,
        in_specs=(P(None, "col", "row"), P(None, ("row", "col")), P(None, "col")),
        out_specs=(P(), P(None, ("row", "col"))),
        check_vma=False,
    )
```

profile of v0, /device:TPU:24, one launch (start us, length us, event | category | flops | bytes accessed | tf_op | source)
XLA Modules:
  0.0 230.3 jit_solution(6707584524099942496)
XLA Ops:
  0.6 1.0 fusion.20
  1.6 1.0 fusion.19
  2.6 22.6 %shard_map.50 = bf16[64,16,64]{2,1,0:T(8,128)(2,1)} custom-call(bf16[16,64]{1,0:T(8,128)(2,1)} %bitcast.80), custom_call_target="tpu_custom_call" | custom-call | tf_op jit(solution)/shard_map/pallas_call | solution.py:208
  25.2 1.3 convert_bitcast_fusion.second_t_ref
  26.5 9.5 %shard_map.51 = f32[128,64]{1,0:T(8,128)} custom-call(bf16[1024,64]{1,0:T(8,128)(2,1)} %bitcast.69, f32[48,64]{1,0:T(8,128)} %convert_bitcast_fusion.second_t_ref, bf16[128,48,1024]{2,1,0:T(8,128)(2,1)} %slab_ref.7), custom_call_target="tpu_custom_call" | custom-call | flops 805306368 | bytes 12582912 | tf_op jit(solution)/shard_map/pallas_call | solution.py:64
  36.9 11.5 %psum.21 = f32[64,192]{0,1:T(8,128)S(1)} all-reduce(f32[64,192]{0,1:T(8,128)S(1)} %pad_maximum_fusion.1), channel_id=1, replica_groups=mesh['row'=4,'col'=64] {'row'}, use_global_device_ids=true, to_apply=%region_0.0 | all-reduce | flops 12288 | bytes 98304 | tf_op jit(solution)/shard_map/psum | solution.py:244
  49.1 26.7 %shard_map.52 = f32[64,4,64]{2,1,0:T(4,128)} custom-call(f32[64,4,64]{2,1,0:T(4,128)} %bitcast.74), custom_call_target="tpu_custom_call" | custom-call | tf_op jit(solution)/shard_map/pallas_call | solution.py:208
  75.8 1.0 copy.23
  77.1 5.9 %cholesky.59 = f32[64,64]{1,0:T(8,128)S(1)} custom-call(f32[64,64]{1,0:T(8,128)S(1)} %copy.25), custom_call_target="Cholesky" | custom-call | tf_op jit(solution)/shard_map/jit(cholesky)/cholesky | solution.py:16
  84.3 4.9 %custom-call.17 = f32[1,64,64]{1,2,0:T(8,128)S(1)} custom-call(f32[1,64,64]{2,1,0:T(8,128)S(1)} %fusion.1), custom_call_target="InvertDiagBlocksLowerTriangular" | custom-call | tf_op jit(solution)/shard_map/triangular_solve | solution.py:18
  91.3 9.9 %shard_map.53 = f32[64,1024]{1,0:T(8,128)} custom-call(f32[64,128]{1,0:T(8,128)} %fusion.15.frames_ref, f32[64,768]{1,0:T(8,128)} %tile.9.tiled_ref, bf16[128,48,1024]{2,1,0:T(8,128)(2,1)} %slab_ref.7), custom_call_target="tpu_custom_call" | custom-call | flops 805306368 | bytes 12582912 | tf_op jit(solution)/shard_map/pallas_call | solution.py:126
  101.2 1.9 copy.29
  103.1 21.9 %shard_map.54 = f32[16,64]{1,0:T(8,128)} custom-call(f32[64,16,64]{2,1,0:T(8,128)} %bitcast.64), custom_call_target="tpu_custom_call" | custom-call | tf_op jit(solution)/shard_map/pallas_call | solution.py:208
  125.4 5.9 %cholesky.70 = f32[64,64]{1,0:T(8,128)S(1)} custom-call(f32[64,64]{1,0:T(8,128)S(1)} %copy.27), custom_call_target="Cholesky" | custom-call | tf_op jit(solution)/shard_map/jit(cholesky)/cholesky | solution.py:16
  132.6 4.9 %custom-call.18 = f32[1,64,64]{1,2,0:T(8,128)S(1)} custom-call(f32[1,64,64]{2,1,0:T(8,128)S(1)} %fusion.2), custom_call_target="InvertDiagBlocksLowerTriangular" | custom-call | tf_op jit(solution)/shard_map/triangular_solve | solution.py:18
  139.3 17.1 %shard_map.55 = bf16[64,16,64]{2,1,0:T(8,128)(2,1)} custom-call(bf16[16,64]{1,0:T(8,128)(2,1)} %convolution_convert_fusion.send_ref), custom_call_target="tpu_custom_call" | custom-call | tf_op jit(solution)/shard_map/pallas_call | solution.py:208
  157.1 9.9 %shard_map.56 = f32[48,64]{1,0:T(8,128)} custom-call(bf16[1024,64]{1,0:T(8,128)(2,1)} %bitcast.68, f32[128,64]{1,0:T(8,128)} %bitcast.77, bf16[128,48,1024]{2,1,0:T(8,128)(2,1)} %slab_ref.7), custom_call_target="tpu_custom_call" | custom-call | flops 805306368 | bytes 12582912 | tf_op jit(solution)/shard_map/pallas_call | solution.py:80
  167.2 11.4 %all-reduce = (f32[64,48]{0,1:T(8,128)S(1)}, f32[64,64]{1,0:T(8,128)S(1)}) all-reduce(f32[64,48]{0,1:T(8,128)} %bitcast.78, f32[64,64]{1,0:T(8,128)S(1)} %convolution_bitcast_fusion), channel_id=1, replica_groups=mesh['row'=4,'col'=64] {'row'}, use_global_device_ids=true, to_apply=%region_4.6 | all-reduce | flops 7168 | bytes 57344 | tf_op jit(solution)/shard_map/psum | solution.py:259
  178.8 5.9 %cholesky.81 = f32[64,64]{1,0:T(8,128)S(1)} custom-call(f32[64,64]{1,0:T(8,128)S(1)} %copy.33), custom_call_target="Cholesky" | custom-call | tf_op jit(solution)/shard_map/jit(cholesky)/cholesky | solution.py:16
  186.0 4.9 %custom-call.19 = f32[1,64,64]{1,2,0:T(8,128)S(1)} custom-call(f32[1,64,64]{2,1,0:T(8,128)S(1)} %fusion.3), custom_call_target="InvertDiagBlocksLowerTriangular" | custom-call | tf_op jit(solution)/shard_map/triangular_solve | solution.py:18
  192.3 9.9 %shard_map.57 = f32[64,1024]{1,0:T(8,128)} custom-call(f32[64,128]{1,0:T(8,128)} %fusion.15.frames_ref, f32[64,768]{1,0:T(8,128)} %tile.21.tiled_ref, bf16[128,48,1024]{2,1,0:T(8,128)(2,1)} %slab_ref.7), custom_call_target="tpu_custom_call" | custom-call | flops 805306368 | bytes 12582912 | tf_op jit(solution)/shard_map/pallas_call | solution.py:126
  202.1 1.9 copy.36
  204.1 24.9 %shard_map.58 = f32[16,64]{1,0:T(8,128)} custom-call(f32[64,16,64]{2,1,0:T(8,128)} %bitcast.65), custom_call_target="tpu_custom_call" | custom-call | tf_op jit(solution)/shard_map/pallas_call | solution.py:208
  229.0 1.3 copy.43
  (42 shorter events, 12.4 us)
Async XLA Ops:
  0.6 89.6 %copy-start.2 = (bf16[64,48]{0,1:T(8,128)(2,1)S(1)}, bf16[64,48]{0,1:T(8,128)(2,1)}, u32[]{:S(2)}) copy-start(bf16[64,48]{0,1:T(8,128)(2,1)} %param.6) | copy-start | bytes 18436
  90.3 34.8 %copy-start = (f32[64,128]{1,0:T(8,128)S(1)}, f32[64,128]{1,0:T(8,128)}, u32[]{:S(2)}) copy-start(f32[64,128]{1,0:T(8,128)} %fusion.15.frames_ref) | copy-start | bytes 98308
  156.4 10.6 %copy-start.1 = (bf16[64,16,64]{2,1,0:T(8,128)(2,1)S(1)}, bf16[64,16,64]{2,1,0:T(8,128)(2,1)}, u32[]{:S(2)}) copy-start(bf16[64,16,64]{2,1,0:T(8,128)(2,1)} %shard_map.55) | copy-start | bytes 393220
where the time goes:
time: 233 us; the launch traced here: 230 us
  Pallas kernels  152 us (65%)
  other arithmetic  39.2 us (17%)
  blocking collectives  22.9 us (10%)
  local copies, waits for them, and re-layouts  9.29 us (4%)
  matrix products  5.6 us (2%)
    pallas_call x5, Pallas kernels, col_exchange(): pl.pallas_call(functools.partial(_exchange_kernel, n, mode), out_shape=ja...  113 us
    pallas_call x2, Pallas kernels, accumulate_pass(): pl.pallas_call(_accumulate_kernel, grid=(frame_count // STREAM_FRAMES,),...  19.7 us
    another operation x9, other arithmetic, ridge_solve(): jnp.linalg.cholesky(gram + ridge_weight * jnp.eye(order_size, dtype=jnp.f...  19.6 us
    another operation x6, other arithmetic, ridge_solve(): lax.linalg.triangular_solve(factor_low, middle, left_side=True, lower=Tru...  16.6 us
    psum x1, blocking collectives, local(): lax.psum(jnp.concatenate([frame_part, gram_first_part], axis=1), 'row')  11.5 us
    psum x1, blocking collectives, local(): second_sum, gram_new = lax.psum((second_part, gram_new_part), 'row')  11.4 us
    pallas_call x1, Pallas kernels, second_pass(): pl.pallas_call(_second_kernel, grid=(frame_count // STREAM_FRAMES,), in_s...  9.87 us
    pallas_call x1, Pallas kernels, frame_pass(): pl.pallas_call(_frame_kernel, grid=(frame_count // STREAM_FRAMES,), in_sp...  9.54 us

commit v1 on v0

--- a/solution.py
+++ b/solution.py
@@ -136,77 +136,105 @@
     )(frames, tiled, tensor)
 
 
-def _exchange_kernel(n, mode, send_ref, out_ref, recv, send_sems, recv_sems, *extra):
+def _exchange_kernel(n, rows, mode, send_ref, out_ref, recv, send_sems, recv_sems, *extra):
     me = lax.axis_index("col")
     row = lax.axis_index("row")
-    broadcast = mode == "gather"
-
-    def exchange(source, landing, sends, recvs):
+
+    def exchange(count, mine, device, source, landing, sends, recvs):
         def descriptor(peer, slot):
             return pltpu.make_async_remote_copy(
                 src_ref=source(peer),
                 dst_ref=landing.at[slot],
                 send_sem=sends.at[peer],
                 recv_sem=recvs.at[slot],
-                device_id=(row, peer),
+                device_id=device(peer),
                 device_id_type=MESH_ID,
             )
 
         def start(t, carry):
-            peer = lax.rem(me + 1 + t, n)
-            descriptor(peer, me).start()
+            peer = lax.rem(mine + 1 + t, count)
+            descriptor(peer, mine).start()
             return carry
 
-        lax.fori_loop(0, n - 1, start, 0)
+        lax.fori_loop(0, count - 1, start, 0)
 
         def finish(t, carry):
-            peer = lax.rem(me + 1 + t, n)
+            peer = lax.rem(mine + 1 + t, count)
             copy = descriptor(peer, peer)
             copy.wait_send()
             copy.wait_recv()
             return carry
 
-        lax.fori_loop(0, n - 1, finish, 0)
-        landing[me] = source(me)[...]
+        lax.fori_loop(0, count - 1, finish, 0)
+        landing[mine] = source(mine)[...]
+
+    def along_col(peer):
+        return (row, peer)
+
+    def along_row(peer):
+        return (peer, me)
 
     barrier = pltpu.get_barrier_semaphore()
-
-    def greet(t, carry):
-        peer = lax.rem(me + 1 + t, n)
-        pl.semaphore_signal(barrier, inc=1, device_id=(row, peer), device_id_type=MESH_ID)
-        return carry
-
-    lax.fori_loop(0, n - 1, greet, 0)
-    pl.semaphore_wait(barrier, n - 1)
-    exchange((lambda peer: send_ref) if broadcast else (lambda peer: send_ref.at[peer]), recv, send_sems, recv_sems)
+    greeted = 0
+    for count, mine, device in ((n, me, along_col), (rows, row, along_row)):
+        if (count == n) == (mode == "rowsum") and not (mode == "allreduce" and count == rows):
+            continue
+
+        def greet(t, carry, count=count, mine=mine, device=device):
+            peer = lax.rem(mine + 1 + t, count)
+            pl.semaphore_signal(barrier, inc=1, device_id=device(peer), device_id_type=MESH_ID)
+            return carry
+
+        lax.fori_loop(0, count - 1, greet, 0)
+        greeted += count - 1
+    pl.semaphore_wait(barrier, greeted)
+
+    if mode == "rowsum":
+        exchange(rows, row, along_row, lambda peer: send_ref, recv, send_sems, recv_sems)
+        out_ref[...] = jnp.sum(recv[...], axis=0)
+        return
+    broadcast = mode == "gather"
+    exchange(
+        n, me, along_col, (lambda peer: send_ref) if broadcast else (lambda peer: send_ref.at[peer]),
+        recv, send_sems, recv_sems,
+    )
     if mode == "gather":
         out_ref[...] = recv[...]
     elif mode == "scatter":
         out_ref[...] = jnp.sum(recv[...], axis=0)
     else:
-        chunk, recv_back, back_send_sems, back_recv_sems = extra
+        (chunk, row_recv, row_send_sems, row_recv_sems, total,
+         recv_back, back_send_sems, back_recv_sems) = extra
         chunk[...] = jnp.sum(recv[...], axis=0)
-        exchange(lambda peer: chunk, recv_back, back_send_sems, back_recv_sems)
+        exchange(rows, row, along_row, lambda peer: chunk, row_recv, row_send_sems, row_recv_sems)
+        total[...] = jnp.sum(row_recv[...], axis=0)
+        exchange(n, me, along_col, lambda peer: total, recv_back, back_send_sems, back_recv_sems)
         out_ref[...] = recv_back[...]
 
 
 def col_exchange(send, n, mode, collective_id):
-    piece = tuple(send.shape) if mode == "gather" else tuple(send.shape[1:])
-    out_shape = piece if mode == "scatter" else (n,) + piece
+    rows = lax.axis_size("row")
+    piece = tuple(send.shape) if mode in ("gather", "rowsum") else tuple(send.shape[1:])
+    slots = rows if mode == "rowsum" else n
+    out_shape = piece if mode in ("scatter", "rowsum") else (n,) + piece
     scratch = [
-        pltpu.VMEM((n,) + piece, send.dtype),
-        pltpu.SemaphoreType.DMA((n,)),
-        pltpu.SemaphoreType.DMA((n,)),
+        pltpu.VMEM((slots,) + piece, send.dtype),
+        pltpu.SemaphoreType.DMA((slots,)),
+        pltpu.SemaphoreType.DMA((slots,)),
     ]
     if mode == "allreduce":
         scratch += [
+            pltpu.VMEM(piece, send.dtype),
+            pltpu.VMEM((rows,) + piece, send.dtype),
+            pltpu.SemaphoreType.DMA((rows,)),
+            pltpu.SemaphoreType.DMA((rows,)),
             pltpu.VMEM(piece, send.dtype),
             pltpu.VMEM((n,) + piece, send.dtype),
             pltpu.SemaphoreType.DMA((n,)),
             pltpu.SemaphoreType.DMA((n,)),
         ]
     return pl.pallas_call(
-        functools.partial(_exchange_kernel, n, mode),
+        functools.partial(_exchange_kernel, n, rows, mode),
         out_shape=jax.ShapeDtypeStruct(out_shape, send.dtype),
         in_specs=[pl.BlockSpec(memory_space=pltpu.VMEM)],
         out_specs=pl.BlockSpec(memory_space=pltpu.VMEM),
@@ -226,10 +254,14 @@
     return summed_t.T
 
 
-def col_all_reduce(full, n, collective_id):
+def all_reduce(full, n, collective_id):
     width = full.shape[1] // n
     summed_t = col_exchange(full.T.reshape(n, width, full.shape[0]), n, "allreduce", collective_id)
     return summed_t.reshape(n * width, full.shape[0]).T
+
+
+def row_sum(piece, n, collective_id):
+    return col_exchange(piece, n, "rowsum", collective_id)
 
 
 def local(tensor, first_factor, second_factor):
@@ -241,8 +273,8 @@
     gram_second_part = gram_of(second_factor)
     block_t = col_gather_t(first_factor.T, n)
     frame_part = frame_pass(tensor, block_t, second_values.T).T
-    row_summed = lax.psum(jnp.concatenate([frame_part, gram_first_part], axis=1), "row")
-    summed = col_all_reduce(jnp.concatenate([row_summed, gram_second_part], axis=1), n, 3)
+    scaled_second = gram_second_part * (1.0 / lax.axis_size("row"))
+    summed = all_reduce(jnp.concatenate([frame_part, gram_first_part, scaled_second], axis=1), n, 3)
     frame_sum = summed[:, :frame_count]
     gram_first = summed[:, frame_count:frame_count + components]
     gram_second = summed[:, frame_count + components:]
@@ -255,8 +287,10 @@
     gram_new_part = lax.dot_general(
         new_block_t, new_block_t, (((0,), (0,)), ((), ())), preferred_element_type=jnp.float32
     )
-    second_part = second_pass(tensor, new_block_t, frames.T).T
-    second_sum, gram_new = lax.psum((second_part, gram_new_part), "row")
+    second_part_t = second_pass(tensor, new_block_t, frames.T)
+    summed_new = row_sum(jnp.concatenate([second_part_t, gram_new_part], axis=0), n, 4)
+    second_sum = summed_new[:col_count].T
+    gram_new = summed_new[col_count:]
     new_second = ridge_solve(gram_new * gram_frames, second_sum)
     full_next = accumulate_pass(tensor, frames, new_second)
     mode_one = col_reduce_scatter(full_next, n, 2)

time: 233 us -> 224 us (0.961)
  blocking collectives: 22.9 us -> 0 us
  Pallas kernels: 152 us -> 165 us
    psum x2 -> x0, blocking collectives: 22.9 us -> none  [the longest x1 11.5 us: local(): lax.psum(jnp.concatenate([frame_part, gram_first_part], axis=1), 'row')]
    pallas_call x5 -> x6, Pallas kernels: 113 us -> 126 us  [col_exchange(): pl.pallas_call(functools.partial(_exchange_kernel, n, rows, mode), out_sh...]
where the time goes in v1:
time: 224 us; the launch traced here: 221 us
  Pallas kernels  165 us (74%)
  other arithmetic  41.4 us (18%)
  local copies, waits for them, and re-layouts  10.1 us (5%)
  matrix products  4.13 us (2%)
    pallas_call x6, Pallas kernels, col_exchange(): pl.pallas_call(functools.partial(_exchange_kernel, n, rows, mode), out_sh...  126 us
    pallas_call x2, Pallas kernels, accumulate_pass(): pl.pallas_call(_accumulate_kernel, grid=(frame_count // STREAM_FRAMES,),...  19.7 us
    another operation x9, other arithmetic, ridge_solve(): jnp.linalg.cholesky(gram + ridge_weight * jnp.eye(order_size, dtype=jnp.f...  19.6 us
    another operation x6, other arithmetic, ridge_solve(): lax.linalg.triangular_solve(factor_low, middle, left_side=True, lower=Tru...  16.6 us
    pallas_call x1, Pallas kernels, second_pass(): pl.pallas_call(_second_kernel, grid=(frame_count // STREAM_FRAMES,), in_s...  9.6 us
    pallas_call x1, Pallas kernels, frame_pass(): pl.pallas_call(_frame_kernel, grid=(frame_count // STREAM_FRAMES,), in_sp...  9.54 us

profile of v1, /device:TPU:24, one launch (start us, length us, event | category | flops | bytes accessed | tf_op | source)
XLA Modules:
  0.0 221.2 jit_solution(17574347519868047962)
XLA Ops:
  0.7 22.7 %shard_map.50 = bf16[64,16,64]{2,1,0:T(8,128)(2,1)} custom-call(bf16[16,64]{1,0:T(8,128)(2,1)} %bitcast.77), custom_call_target="tpu_custom_call" | custom-call | tf_op jit(solution)/shard_map/pallas_call | solution.py:236
  23.3 1.3 convert_bitcast_fusion.second_t_ref
  24.7 9.5 %shard_map.51 = f32[128,64]{1,0:T(8,128)} custom-call(bf16[1024,64]{1,0:T(8,128)(2,1)} %bitcast.67, f32[48,64]{1,0:T(8,128)} %convert_bitcast_fusion.second_t_ref, bf16[128,48,1024]{2,1,0:T(8,128)(2,1)} %slab_ref.7), custom_call_target="tpu_custom_call" | custom-call | flops 805306368 | bytes 12582912 | tf_op jit(solution)/shard_map/pallas_call | solution.py:64
  34.6 1.5 pad_maximum_fusion
  36.1 30.5 %shard_map.52 = f32[64,4,64]{2,1,0:T(4,128)} custom-call(f32[64,4,64]{2,1,0:T(4,128)} %bitcast.72), custom_call_target="tpu_custom_call" | custom-call | tf_op jit(solution)/shard_map/pallas_call | solution.py:236
  67.9 5.9 %cholesky.59 = f32[64,64]{1,0:T(8,128)S(1)} custom-call(f32[64,64]{1,0:T(8,128)S(1)} %copy.26), custom_call_target="Cholesky" | custom-call | tf_op jit(solution)/shard_map/jit(cholesky)/cholesky | solution.py:16
  75.1 4.9 %custom-call.17 = f32[1,64,64]{1,2,0:T(8,128)S(1)} custom-call(f32[1,64,64]{2,1,0:T(8,128)S(1)} %fusion.1), custom_call_target="InvertDiagBlocksLowerTriangular" | custom-call | tf_op jit(solution)/shard_map/triangular_solve | solution.py:18
  80.8 5.9 %cholesky.70 = f32[64,64]{1,0:T(8,128)S(1)} custom-call(f32[64,64]{1,0:T(8,128)S(1)} %copy.28), custom_call_target="Cholesky" | custom-call | tf_op jit(solution)/shard_map/jit(cholesky)/cholesky | solution.py:16
  88.0 4.9 %custom-call.18 = f32[1,64,64]{1,2,0:T(8,128)S(1)} custom-call(f32[1,64,64]{2,1,0:T(8,128)S(1)} %fusion.2), custom_call_target="InvertDiagBlocksLowerTriangular" | custom-call | tf_op jit(solution)/shard_map/triangular_solve | solution.py:18
  93.9 9.9 %shard_map.53 = f32[64,1024]{1,0:T(8,128)} custom-call(f32[64,128]{1,0:T(8,128)} %copy-done, f32[64,768]{1,0:T(8,128)} %tile.9.tiled_ref, bf16[128,48,1024]{2,1,0:T(8,128)(2,1)} %slab_ref.7), custom_call_target="tpu_custom_call" | custom-call | flops 805306368 | bytes 12582912 | tf_op jit(solution)/shard_map/pallas_call | solution.py:126
  103.8 1.9 copy.30
  105.7 23.6 %shard_map.54 = f32[16,64]{1,0:T(8,128)} custom-call(f32[64,16,64]{2,1,0:T(8,128)} %bitcast.62), custom_call_target="tpu_custom_call" | custom-call | tf_op jit(solution)/shard_map/pallas_call | solution.py:236
  131.1 17.8 %shard_map.55 = bf16[64,16,64]{2,1,0:T(8,128)(2,1)} custom-call(bf16[16,64]{1,0:T(8,128)(2,1)} %convolution_convert_fusion.send_ref), custom_call_target="tpu_custom_call" | custom-call | tf_op jit(solution)/shard_map/pallas_call | solution.py:236
  148.9 1.5 copy.31
  150.4 9.6 %shard_map.56 = f32[48,64]{1,0:T(8,128)} custom-call(bf16[1024,64]{1,0:T(8,128)(2,1)} %bitcast.66, f32[128,64]{1,0:T(8,128)} %bitcast.74, bf16[128,48,1024]{2,1,0:T(8,128)(2,1)} %slab_ref.7), custom_call_target="tpu_custom_call" | custom-call | flops 805306368 | bytes 12582912 | tf_op jit(solution)/shard_map/pallas_call | solution.py:80
  160.2 1.4 pad_maximum_fusion.1.send_ref
  161.6 6.3 %shard_map.57 = f32[112,64]{1,0:T(8,128)} custom-call(f32[112,64]{1,0:T(8,128)} %pad_maximum_fusion.1.send_ref), custom_call_target="tpu_custom_call" | custom-call | tf_op jit(solution)/shard_map/pallas_call | solution.py:236
  168.8 5.9 %cholesky.81 = f32[64,64]{1,0:T(8,128)S(1)} custom-call(f32[64,64]{1,0:T(8,128)S(1)} %copy.36), custom_call_target="Cholesky" | custom-call | tf_op jit(solution)/shard_map/jit(cholesky)/cholesky | solution.py:16
  176.0 4.9 %custom-call.19 = f32[1,64,64]{1,2,0:T(8,128)S(1)} custom-call(f32[1,64,64]{2,1,0:T(8,128)S(1)} %fusion.3), custom_call_target="InvertDiagBlocksLowerTriangular" | custom-call | tf_op jit(solution)/shard_map/triangular_solve | solution.py:18
  180.9 1.0 fusion.8
  183.0 9.9 %shard_map.58 = f32[64,1024]{1,0:T(8,128)} custom-call(f32[64,128]{1,0:T(8,128)} %copy-done, f32[64,768]{1,0:T(8,128)} %tile.21.tiled_ref, bf16[128,48,1024]{2,1,0:T(8,128)(2,1)} %slab_ref.7), custom_call_target="tpu_custom_call" | custom-call | flops 805306368 | bytes 12582912 | tf_op jit(solution)/shard_map/pallas_call | solution.py:126
  192.9 1.9 copy.38
  194.8 25.1 %shard_map.59 = f32[16,64]{1,0:T(8,128)} custom-call(f32[64,16,64]{2,1,0:T(8,128)} %bitcast.63), custom_call_target="tpu_custom_call" | custom-call | tf_op jit(solution)/shard_map/pallas_call | solution.py:236
  219.9 1.3 copy.47
  (43 shorter events, 11.5 us)
Async XLA Ops:
  0.6 33.8 %copy-start.3 = (bf16[64,16]{0,1:T(8,128)(2,1)S(1)}, bf16[64,16]{0,1:T(8,128)(2,1)}, u32[]{:S(2)}) copy-start(bf16[64,16]{0,1:T(8,128)(2,1)} %param.5) | copy-start | bytes 6148
  0.6 33.6 %copy-start.2 = (bf16[64,48]{0,1:T(8,128)(2,1)S(1)}, bf16[64,48]{0,1:T(8,128)(2,1)}, u32[]{:S(2)}) copy-start(bf16[64,48]{0,1:T(8,128)(2,1)} %param.6) | copy-start | bytes 18436
  80.4 13.5 %copy-start = (f32[64,128]{1,0:T(8,128)}, f32[64,128]{1,0:T(8,128)S(1)}, u32[]{:S(2)}) copy-start(f32[64,128]{1,0:T(8,128)S(1)} %fusion.15.frames_ref) | copy-start | bytes 98308
  148.9 11.1 %copy-start.1 = (bf16[64,16,64]{2,1,0:T(8,128)(2,1)S(1)}, bf16[64,16,64]{2,1,0:T(8,128)(2,1)}, u32[]{:S(2)}) copy-start(bf16[64,16,64]{2,1,0:T(8,128)(2,1)} %shard_map.55) | copy-start | bytes 393220

commit v2 on v1

--- a/solution.py
+++ b/solution.py
@@ -136,9 +136,26 @@
     )(frames, tiled, tensor)
 
 
-def _exchange_kernel(n, rows, mode, send_ref, out_ref, recv, send_sems, recv_sems, *extra):
+def _split(n):
+    inner = next(d for d in (8, 4, 2, 1) if n % d == 0 and d * d <= n)
+    return inner, n // inner
+
+
+def _exchange_kernel(n, rows, mode, send_ref, out_ref, *scratch):
     me = lax.axis_index("col")
     row = lax.axis_index("row")
+    inner, outer = _split(n)
+    low = lax.rem(me, inner)
+    high = me // inner
+
+    def in_low(peer):
+        return (row, high * inner + peer)
+
+    def in_high(peer):
+        return (row, peer * inner + low)
+
+    def in_row(peer):
+        return (peer, me)
 
     def exchange(count, mine, device, source, landing, sends, recvs):
         def descriptor(peer, slot):
@@ -168,74 +185,90 @@
         lax.fori_loop(0, count - 1, finish, 0)
         landing[mine] = source(mine)[...]
 
-    def along_col(peer):
-        return (row, peer)
-
-    def along_row(peer):
-        return (peer, me)
-
+    if mode == "rowsum":
+        groups = [(rows, row, in_row)]
+    else:
+        groups = [(inner, low, in_low), (outer, high, in_high)]
+        if mode == "allreduce":
+            groups.append((rows, row, in_row))
     barrier = pltpu.get_barrier_semaphore()
-    greeted = 0
-    for count, mine, device in ((n, me, along_col), (rows, row, along_row)):
-        if (count == n) == (mode == "rowsum") and not (mode == "allreduce" and count == rows):
-            continue
-
+    for count, mine, device in groups:
         def greet(t, carry, count=count, mine=mine, device=device):
             peer = lax.rem(mine + 1 + t, count)
             pl.semaphore_signal(barrier, inc=1, device_id=device(peer), device_id_type=MESH_ID)
             return carry
 
         lax.fori_loop(0, count - 1, greet, 0)
-        greeted += count - 1
-    pl.semaphore_wait(barrier, greeted)
+    pl.semaphore_wait(barrier, sum(count - 1 for count, _, _ in groups))
+
+    scratch = list(scratch)
+
+    def take(k):
+        taken = scratch[:k]
+        del scratch[:k]
+        return taken
+
+    def gather(piece_ref):
+        bundle, s1, r1 = take(3)
+        exchange(outer, high, in_high, lambda peer: piece_ref, bundle, s1, r1)
+        everything, s2, r2 = take(3)
+        exchange(inner, low, in_low, lambda peer: bundle, everything, s2, r2)
+        out_ref[...] = everything[...]
 
     if mode == "rowsum":
-        exchange(rows, row, along_row, lambda peer: send_ref, recv, send_sems, recv_sems)
-        out_ref[...] = jnp.sum(recv[...], axis=0)
+        landing, s1, r1 = take(3)
+        exchange(rows, row, in_row, lambda peer: send_ref, landing, s1, r1)
+        out_ref[...] = jnp.sum(landing[...], axis=0)
         return
-    broadcast = mode == "gather"
-    exchange(
-        n, me, along_col, (lambda peer: send_ref) if broadcast else (lambda peer: send_ref.at[peer]),
-        recv, send_sems, recv_sems,
-    )
     if mode == "gather":
-        out_ref[...] = recv[...]
-    elif mode == "scatter":
-        out_ref[...] = jnp.sum(recv[...], axis=0)
-    else:
-        (chunk, row_recv, row_send_sems, row_recv_sems, total,
-         recv_back, back_send_sems, back_recv_sems) = extra
-        chunk[...] = jnp.sum(recv[...], axis=0)
-        exchange(rows, row, along_row, lambda peer: chunk, row_recv, row_send_sems, row_recv_sems)
-        total[...] = jnp.sum(row_recv[...], axis=0)
-        exchange(n, me, along_col, lambda peer: total, recv_back, back_send_sems, back_recv_sems)
-        out_ref[...] = recv_back[...]
+        gather(send_ref)
+        return
+    landing, s1, r1, partial = take(4)
+    exchange(inner, low, in_low, lambda peer: send_ref.at[peer], landing, s1, r1)
+    partial[...] = jnp.sum(landing[...], axis=0)
+    landing2, s2, r2 = take(3)
+    exchange(outer, high, in_high, lambda peer: partial.at[peer], landing2, s2, r2)
+    if mode == "scatter":
+        out_ref[...] = jnp.sum(landing2[...], axis=0)
+        return
+    chunk, row_landing, s3, r3, total = take(5)
+    chunk[...] = jnp.sum(landing2[...], axis=0)
+    exchange(rows, row, in_row, lambda peer: chunk, row_landing, s3, r3)
+    total[...] = jnp.sum(row_landing[...], axis=0)
+    gather(total)
 
 
 def col_exchange(send, n, mode, collective_id):
     rows = lax.axis_size("row")
-    piece = tuple(send.shape) if mode in ("gather", "rowsum") else tuple(send.shape[1:])
-    slots = rows if mode == "rowsum" else n
-    out_shape = piece if mode in ("scatter", "rowsum") else (n,) + piece
-    scratch = [
-        pltpu.VMEM((slots,) + piece, send.dtype),
-        pltpu.SemaphoreType.DMA((slots,)),
-        pltpu.SemaphoreType.DMA((slots,)),
-    ]
-    if mode == "allreduce":
-        scratch += [
-            pltpu.VMEM(piece, send.dtype),
-            pltpu.VMEM((rows,) + piece, send.dtype),
-            pltpu.SemaphoreType.DMA((rows,)),
-            pltpu.SemaphoreType.DMA((rows,)),
-            pltpu.VMEM(piece, send.dtype),
-            pltpu.VMEM((n,) + piece, send.dtype),
-            pltpu.SemaphoreType.DMA((n,)),
-            pltpu.SemaphoreType.DMA((n,)),
+    inner, outer = _split(n)
+    dtype = send.dtype
+
+    def stage(count, piece):
+        return [
+            pltpu.VMEM((count,) + piece, dtype),
+            pltpu.SemaphoreType.DMA((count,)),
+            pltpu.SemaphoreType.DMA((count,)),
         ]
+
+    if mode == "rowsum":
+        piece = tuple(send.shape)
+        out_shape = piece
+        scratch = stage(rows, piece)
+    elif mode == "gather":
+        piece = tuple(send.shape)
+        out_shape = (inner, outer) + piece
+        scratch = stage(outer, piece) + stage(inner, (outer,) + piece)
+    else:
+        piece = tuple(send.shape[2:])
+        out_shape = piece if mode == "scatter" else (inner, outer) + piece
+        scratch = stage(inner, (outer,) + piece) + [pltpu.VMEM((outer,) + piece, dtype)]
+        scratch += stage(outer, piece)
+        if mode == "allreduce":
+            scratch += [pltpu.VMEM(piece, dtype)] + stage(rows, piece) + [pltpu.VMEM(piece, dtype)]
+            scratch += stage(outer, piece) + stage(inner, (outer,) + piece)
     return pl.pallas_call(
         functools.partial(_exchange_kernel, n, rows, mode),
-        out_shape=jax.ShapeDtypeStruct(out_shape, send.dtype),
+        out_shape=jax.ShapeDtypeStruct(out_shape, dtype),
         in_specs=[pl.BlockSpec(memory_space=pltpu.VMEM)],
         out_specs=pl.BlockSpec(memory_space=pltpu.VMEM),
         scratch_shapes=scratch,
@@ -243,20 +276,30 @@
     )(send)
 
 
+def _chunk_order(chunks, n):
+    inner, outer = _split(n)
+    return chunks.reshape((outer, inner) + chunks.shape[1:]).swapaxes(0, 1)
+
+
+def _col_order(gathered, n):
+    return gathered.swapaxes(0, 1).reshape((n,) + gathered.shape[2:])
+
+
 def col_gather_t(piece_t, n):
-    gathered = col_exchange(piece_t, n, "gather", 0)
+    gathered = _col_order(col_exchange(piece_t, n, "gather", 0), n)
     return gathered.reshape(n * piece_t.shape[0], piece_t.shape[1])
 
 
 def col_reduce_scatter(full, n, collective_id):
     width = full.shape[1] // n
-    summed_t = col_exchange(full.T.reshape(n, width, full.shape[0]), n, "scatter", collective_id)
-    return summed_t.T
+    chunks = _chunk_order(full.T.reshape(n, width, full.shape[0]), n)
+    return col_exchange(chunks, n, "scatter", collective_id).T
 
 
 def all_reduce(full, n, collective_id):
     width = full.shape[1] // n
-    summed_t = col_exchange(full.T.reshape(n, width, full.shape[0]), n, "allreduce", collective_id)
+    chunks = _chunk_order(full.T.reshape(n, width, full.shape[0]), n)
+    summed_t = _col_order(col_exchange(chunks, n, "allreduce", collective_id), n)
     return summed_t.reshape(n * width, full.shape[0]).T
 
 

time: 224 us -> 223 us (level)
  Pallas kernels: 165 us -> 160 us
  local copies, waits for them, and re-layouts: 10.1 us -> 14.3 us
    pallas_call x6, Pallas kernels: 126 us -> 121 us  [col_exchange(): pl.pallas_call(functools.partial(_exchange_kernel, n, rows, mode), out_sh...]
    transpose x2 -> x5, local copies, waits for them, and re-layouts: 3.89 us -> 6.6 us  [the longest x3 4.32 us: _col_order(): return gathered.swapaxes(0, 1).reshape((n,) + gathered.shape[2:])]
    another operation x0 -> x4, local copies, waits for them, and re-layouts: none -> 2.42 us  [the longest x3 2.34 us: _chunk_order(): return chunks.reshape((outer, inner) + chunks.shape[1:]).swapaxes(0, 1)]
where the time goes in v2:
time: 223 us; the launch traced here: 220 us
  Pallas kernels  160 us (72%)
  other arithmetic  40.7 us (18%)
  local copies, waits for them, and re-layouts  14.3 us (6%)
  matrix products  4.12 us (2%)
    pallas_call x6, Pallas kernels, col_exchange(): pl.pallas_call(functools.partial(_exchange_kernel, n, rows, mode), out_sh...  121 us
    pallas_call x2, Pallas kernels, accumulate_pass(): pl.pallas_call(_accumulate_kernel, grid=(frame_count // STREAM_FRAMES,),...  19.7 us
    another operation x9, other arithmetic, ridge_solve(): jnp.linalg.cholesky(gram + ridge_weight * jnp.eye(order_size, dtype=jnp.f...  19.6 us
    another operation x6, other arithmetic, ridge_solve(): lax.linalg.triangular_solve(factor_low, middle, left_side=True, lower=Tru...  16.6 us
    pallas_call x1, Pallas kernels, second_pass(): pl.pallas_call(_second_kernel, grid=(frame_count // STREAM_FRAMES,), in_s...  9.58 us
    pallas_call x1, Pallas kernels, frame_pass(): pl.pallas_call(_frame_kernel, grid=(frame_count // STREAM_FRAMES,), in_sp...  9.55 us

profile of v2, /device:TPU:24, one launch (start us, length us, event | category | flops | bytes accessed | tf_op | source)
XLA Modules:
  0.0 219.7 jit_solution(15424230596866621989)
XLA Ops:
  0.7 21.3 %shard_map.50 = bf16[8,8,16,64]{3,2,1,0:T(8,128)(2,1)} custom-call(bf16[16,64]{1,0:T(8,128)(2,1)} %bitcast.98), custom_call_target="tpu_custom_call" | custom-call | tf_op jit(solution)/shard_map/pallas_call | solution.py:269
  22.0 1.7 copy.22
  23.6 1.3 convert_bitcast_fusion.second_t_ref
  25.0 9.5 %shard_map.51 = f32[128,64]{1,0:T(8,128)} custom-call(bf16[1024,64]{1,0:T(8,128)(2,1)} %bitcast.83, f32[48,64]{1,0:T(8,128)} %convert_bitcast_fusion.second_t_ref, bf16[128,48,1024]{2,1,0:T(8,128)(2,1)} %slab_ref.7), custom_call_target="tpu_custom_call" | custom-call | flops 805306368 | bytes 12582912 | tf_op jit(solution)/shard_map/pallas_call | solution.py:64
  36.4 28.9 %shard_map.52 = f32[8,8,4,64]{3,2,1,0:T(4,128)} custom-call(f32[8,8,4,64]{3,2,1,0:T(4,128)} %bitcast.92), custom_call_target="tpu_custom_call" | custom-call | tf_op jit(solution)/shard_map/pallas_call | solution.py:269
  66.7 5.9 %cholesky.59 = f32[64,64]{1,0:T(8,128)S(1)} custom-call(f32[64,64]{1,0:T(8,128)S(1)} %copy.29), custom_call_target="Cholesky" | custom-call | tf_op jit(solution)/shard_map/jit(cholesky)/cholesky | solution.py:16
  73.9 4.9 %custom-call.17 = f32[1,64,64]{1,2,0:T(8,128)S(1)} custom-call(f32[1,64,64]{2,1,0:T(8,128)S(1)} %fusion), custom_call_target="InvertDiagBlocksLowerTriangular" | custom-call | tf_op jit(solution)/shard_map/triangular_solve | solution.py:18
  79.6 5.9 %cholesky.70 = f32[64,64]{1,0:T(8,128)S(1)} custom-call(f32[64,64]{1,0:T(8,128)S(1)} %copy.31), custom_call_target="Cholesky" | custom-call | tf_op jit(solution)/shard_map/jit(cholesky)/cholesky | solution.py:16
  86.8 4.9 %custom-call.18 = f32[1,64,64]{1,2,0:T(8,128)S(1)} custom-call(f32[1,64,64]{2,1,0:T(8,128)S(1)} %fusion.1), custom_call_target="InvertDiagBlocksLowerTriangular" | custom-call | tf_op jit(solution)/shard_map/triangular_solve | solution.py:18
  92.7 9.9 %shard_map.53 = f32[64,1024]{1,0:T(8,128)} custom-call(f32[64,128]{1,0:T(8,128)} %copy-done, f32[64,768]{1,0:T(8,128)} %tile.9.tiled_ref, bf16[128,48,1024]{2,1,0:T(8,128)(2,1)} %slab_ref.7), custom_call_target="tpu_custom_call" | custom-call | flops 805306368 | bytes 12582912 | tf_op jit(solution)/shard_map/pallas_call | solution.py:126
  102.6 1.1 copy.33
  104.6 22.7 %shard_map.54 = f32[16,64]{1,0:T(8,128)} custom-call(f32[8,8,16,64]{3,2,1,0:T(8,128)} %bitcast.78), custom_call_target="tpu_custom_call" | custom-call | tf_op jit(solution)/shard_map/pallas_call | solution.py:269
  129.0 16.6 %shard_map.55 = bf16[8,8,16,64]{3,2,1,0:T(8,128)(2,1)} custom-call(bf16[16,64]{1,0:T(8,128)(2,1)} %convolution_convert_fusion.send_ref), custom_call_target="tpu_custom_call" | custom-call | tf_op jit(solution)/shard_map/pallas_call | solution.py:269
  145.7 1.7 copy.35
  147.4 1.5 copy.36
  148.9 9.6 %shard_map.56 = f32[48,64]{1,0:T(8,128)} custom-call(bf16[1024,64]{1,0:T(8,128)(2,1)} %bitcast.84, f32[128,64]{1,0:T(8,128)} %bitcast.95, bf16[128,48,1024]{2,1,0:T(8,128)(2,1)} %slab_ref.7), custom_call_target="tpu_custom_call" | custom-call | flops 805306368 | bytes 12582912 | tf_op jit(solution)/shard_map/pallas_call | solution.py:80
  158.7 1.4 pad_maximum_fusion.1.send_ref
  160.1 6.3 %shard_map.57 = f32[112,64]{1,0:T(8,128)} custom-call(f32[112,64]{1,0:T(8,128)} %pad_maximum_fusion.1.send_ref), custom_call_target="tpu_custom_call" | custom-call | tf_op jit(solution)/shard_map/pallas_call | solution.py:269
  167.3 5.9 %cholesky.81 = f32[64,64]{1,0:T(8,128)S(1)} custom-call(f32[64,64]{1,0:T(8,128)S(1)} %copy.41), custom_call_target="Cholesky" | custom-call | tf_op jit(solution)/shard_map/jit(cholesky)/cholesky | solution.py:16
  174.5 4.9 %custom-call.19 = f32[1,64,64]{1,2,0:T(8,128)S(1)} custom-call(f32[1,64,64]{2,1,0:T(8,128)S(1)} %fusion.2), custom_call_target="InvertDiagBlocksLowerTriangular" | custom-call | tf_op jit(solution)/shard_map/triangular_solve | solution.py:18
  181.5 9.9 %shard_map.58 = f32[64,1024]{1,0:T(8,128)} custom-call(f32[64,128]{1,0:T(8,128)} %copy-done, f32[64,768]{1,0:T(8,128)} %tile.21.tiled_ref, bf16[128,48,1024]{2,1,0:T(8,128)(2,1)} %slab_ref.7), custom_call_target="tpu_custom_call" | custom-call | flops 805306368 | bytes 12582912 | tf_op jit(solution)/shard_map/pallas_call | solution.py:126
  191.3 1.1 copy.43
  193.3 25.1 %shard_map.59 = f32[16,64]{1,0:T(8,128)} custom-call(f32[8,8,16,64]{3,2,1,0:T(8,128)} %bitcast.80), custom_call_target="tpu_custom_call" | custom-call | tf_op jit(solution)/shard_map/pallas_call | solution.py:269
  218.4 1.3 copy.59
  (49 shorter events, 15.7 us)
Async XLA Ops:
  0.6 34.1 %copy-start.3 = (bf16[64,16]{0,1:T(8,128)(2,1)S(1)}, bf16[64,16]{0,1:T(8,128)(2,1)}, u32[]{:S(2)}) copy-start(bf16[64,16]{0,1:T(8,128)(2,1)} %param.5) | copy-start | bytes 6148
  0.6 33.9 %copy-start.2 = (bf16[64,48]{0,1:T(8,128)(2,1)S(1)}, bf16[64,48]{0,1:T(8,128)(2,1)}, u32[]{:S(2)}) copy-start(bf16[64,48]{0,1:T(8,128)(2,1)} %param.6) | copy-start | bytes 18436
  79.2 13.5 %copy-start = (f32[64,128]{1,0:T(8,128)}, f32[64,128]{1,0:T(8,128)S(1)}, u32[]{:S(2)}) copy-start(f32[64,128]{1,0:T(8,128)S(1)} %fusion.14.frames_ref) | copy-start | bytes 98308
  145.7 12.8 %copy-start.1 = (bf16[8,8,16,64]{3,2,1,0:T(8,128)(2,1)S(1)}, bf16[8,8,16,64]{3,2,1,0:T(8,128)(2,1)}, u32[]{:S(2)}) copy-start(bf16[8,8,16,64]{3,2,1,0:T(8,128)(2,1)} %shard_map.55) | copy-start | bytes 393220

commit v3 on v2

--- a/solution.py
+++ b/solution.py
@@ -210,9 +210,9 @@
 
     def gather(piece_ref):
         bundle, s1, r1 = take(3)
-        exchange(outer, high, in_high, lambda peer: piece_ref, bundle, s1, r1)
+        exchange(inner, low, in_low, lambda peer: piece_ref, bundle, s1, r1)
         everything, s2, r2 = take(3)
-        exchange(inner, low, in_low, lambda peer: bundle, everything, s2, r2)
+        exchange(outer, high, in_high, lambda peer: bundle, everything, s2, r2)
         out_ref[...] = everything[...]
 
     if mode == "rowsum":
@@ -224,10 +224,10 @@
         gather(send_ref)
         return
     landing, s1, r1, partial = take(4)
-    exchange(inner, low, in_low, lambda peer: send_ref.at[peer], landing, s1, r1)
+    exchange(outer, high, in_high, lambda peer: send_ref.at[peer], landing, s1, r1)
     partial[...] = jnp.sum(landing[...], axis=0)
     landing2, s2, r2 = take(3)
-    exchange(outer, high, in_high, lambda peer: partial.at[peer], landing2, s2, r2)
+    exchange(inner, low, in_low, lambda peer: partial.at[peer], landing2, s2, r2)
     if mode == "scatter":
         out_ref[...] = jnp.sum(landing2[...], axis=0)
         return
@@ -256,16 +256,16 @@
         scratch = stage(rows, piece)
     elif mode == "gather":
         piece = tuple(send.shape)
-        out_shape = (inner, outer) + piece
-        scratch = stage(outer, piece) + stage(inner, (outer,) + piece)
+        out_shape = (outer, inner) + piece
+        scratch = stage(inner, piece) + stage(outer, (inner,) + piece)
     else:
         piece = tuple(send.shape[2:])
-        out_shape = piece if mode == "scatter" else (inner, outer) + piece
-        scratch = stage(inner, (outer,) + piece) + [pltpu.VMEM((outer,) + piece, dtype)]
-        scratch += stage(outer, piece)
+        out_shape = piece if mode == "scatter" else (outer, inner) + piece
+        scratch = stage(outer, (inner,) + piece) + [pltpu.VMEM((inner,) + piece, dtype)]
+        scratch += stage(inner, piece)
         if mode == "allreduce":
             scratch += [pltpu.VMEM(piece, dtype)] + stage(rows, piece) + [pltpu.VMEM(piece, dtype)]
-            scratch += stage(outer, piece) + stage(inner, (outer,) + piece)
+            scratch += stage(inner, piece) + stage(outer, (inner,) + piece)
     return pl.pallas_call(
         functools.partial(_exchange_kernel, n, rows, mode),
         out_shape=jax.ShapeDtypeStruct(out_shape, dtype),
@@ -278,11 +278,11 @@
 
 def _chunk_order(chunks, n):
     inner, outer = _split(n)
-    return chunks.reshape((outer, inner) + chunks.shape[1:]).swapaxes(0, 1)
+    return chunks.reshape((outer, inner) + chunks.shape[1:])
 
 
 def _col_order(gathered, n):
-    return gathered.swapaxes(0, 1).reshape((n,) + gathered.shape[2:])
+    return gathered.reshape((n,) + gathered.shape[2:])
 
 
 def col_gather_t(piece_t, n):

time: 223 us -> 204 us (0.915); the launches traced: 220 us -> 203 us
  Pallas kernels: 160 us -> 147 us
  local copies, waits for them, and re-layouts: 14.3 us -> 10.1 us
    pallas_call x6, Pallas kernels: 121 us -> 108 us  [col_exchange(): pl.pallas_call(functools.partial(_exchange_kernel, n, rows, mode), out_sh...]
    transpose x3 -> x0, local copies, waits for them, and re-layouts: 4.32 us -> none  [_col_order(): return gathered.swapaxes(0, 1).reshape((n,) + gathered.shape[2:])]
    another operation x3 -> x0, local copies, waits for them, and re-layouts: 2.34 us -> none  [_chunk_order(): return chunks.reshape((outer, inner) + chunks.shape[1:]).swapaxes(0, 1)]
where the time goes in v3:
time: 204 us; the launch traced here: 203 us
  Pallas kernels  147 us (72%)
  other arithmetic  41.4 us (20%)
  local copies, waits for them, and re-layouts  10.1 us (5%)
  matrix products  4.12 us (2%)
    pallas_call x6, Pallas kernels, col_exchange(): pl.pallas_call(functools.partial(_exchange_kernel, n, rows, mode), out_sh...  108 us
    pallas_call x2, Pallas kernels, accumulate_pass(): pl.pallas_call(_accumulate_kernel, grid=(frame_count // STREAM_FRAMES,),...  19.7 us
    another operation x9, other arithmetic, ridge_solve(): jnp.linalg.cholesky(gram + ridge_weight * jnp.eye(order_size, dtype=jnp.f...  19.6 us
    another operation x6, other arithmetic, ridge_solve(): lax.linalg.triangular_solve(factor_low, middle, left_side=True, lower=Tru...  16.6 us
    pallas_call x1, Pallas kernels, second_pass(): pl.pallas_call(_second_kernel, grid=(frame_count // STREAM_FRAMES,), in_s...  9.59 us
    pallas_call x1, Pallas kernels, frame_pass(): pl.pallas_call(_frame_kernel, grid=(frame_count // STREAM_FRAMES,), in_sp...  9.55 us

profile of v3, /device:TPU:24, one launch (start us, length us, event | category | flops | bytes accessed | tf_op | source)
XLA Modules:
  0.0 203.3 jit_solution(2063738149503082013)
XLA Ops:
  0.7 20.4 %shard_map.50 = bf16[8,8,16,64]{3,2,1,0:T(8,128)(2,1)} custom-call(bf16[16,64]{1,0:T(8,128)(2,1)} %bitcast.79), custom_call_target="tpu_custom_call" | custom-call | tf_op jit(solution)/shard_map/pallas_call | solution.py:269
  21.1 1.3 convert_bitcast_fusion.second_t_ref
  22.4 9.5 %shard_map.51 = f32[128,64]{1,0:T(8,128)} custom-call(bf16[1024,64]{1,0:T(8,128)(2,1)} %bitcast.69, f32[48,64]{1,0:T(8,128)} %convert_bitcast_fusion.second_t_ref, bf16[128,48,1024]{2,1,0:T(8,128)(2,1)} %slab_ref.7), custom_call_target="tpu_custom_call" | custom-call | flops 805306368 | bytes 12582912 | tf_op jit(solution)/shard_map/pallas_call | solution.py:64
  32.4 1.5 pad_maximum_fusion
  33.9 26.9 %shard_map.52 = f32[8,8,4,64]{3,2,1,0:T(4,128)} custom-call(f32[8,8,4,64]{3,2,1,0:T(4,128)} %bitcast.74), custom_call_target="tpu_custom_call" | custom-call | tf_op jit(solution)/shard_map/pallas_call | solution.py:269
  62.1 5.9 %cholesky.59 = f32[64,64]{1,0:T(8,128)S(1)} custom-call(f32[64,64]{1,0:T(8,128)S(1)} %copy.24), custom_call_target="Cholesky" | custom-call | tf_op jit(solution)/shard_map/jit(cholesky)/cholesky | solution.py:16
  69.3 4.9 %custom-call.17 = f32[1,64,64]{1,2,0:T(8,128)S(1)} custom-call(f32[1,64,64]{2,1,0:T(8,128)S(1)} %fusion), custom_call_target="InvertDiagBlocksLowerTriangular" | custom-call | tf_op jit(solution)/shard_map/triangular_solve | solution.py:18
  75.0 5.9 %cholesky.70 = f32[64,64]{1,0:T(8,128)S(1)} custom-call(f32[64,64]{1,0:T(8,128)S(1)} %copy.26), custom_call_target="Cholesky" | custom-call | tf_op jit(solution)/shard_map/jit(cholesky)/cholesky | solution.py:16
  82.2 4.9 %custom-call.18 = f32[1,64,64]{1,2,0:T(8,128)S(1)} custom-call(f32[1,64,64]{2,1,0:T(8,128)S(1)} %fusion.1), custom_call_target="InvertDiagBlocksLowerTriangular" | custom-call | tf_op jit(solution)/shard_map/triangular_solve | solution.py:18
  88.1 9.9 %shard_map.53 = f32[64,1024]{1,0:T(8,128)} custom-call(f32[64,128]{1,0:T(8,128)} %copy-done, f32[64,768]{1,0:T(8,128)} %tile.9.tiled_ref, bf16[128,48,1024]{2,1,0:T(8,128)(2,1)} %slab_ref.7), custom_call_target="tpu_custom_call" | custom-call | flops 805306368 | bytes 12582912 | tf_op jit(solution)/shard_map/pallas_call | solution.py:126
  98.0 1.9 copy.28
  99.9 18.2 %shard_map.54 = f32[16,64]{1,0:T(8,128)} custom-call(f32[8,8,16,64]{3,2,1,0:T(8,128)} %bitcast.64), custom_call_target="tpu_custom_call" | custom-call | tf_op jit(solution)/shard_map/pallas_call | solution.py:269
  119.9 15.4 %shard_map.55 = bf16[8,8,16,64]{3,2,1,0:T(8,128)(2,1)} custom-call(bf16[16,64]{1,0:T(8,128)(2,1)} %convolution_convert_fusion.send_ref), custom_call_target="tpu_custom_call" | custom-call | tf_op jit(solution)/shard_map/pallas_call | solution.py:269
  135.3 1.5 copy.29
  136.8 9.6 %shard_map.56 = f32[48,64]{1,0:T(8,128)} custom-call(bf16[1024,64]{1,0:T(8,128)(2,1)} %bitcast.68, f32[128,64]{1,0:T(8,128)} %bitcast.76, bf16[128,48,1024]{2,1,0:T(8,128)(2,1)} %slab_ref.7), custom_call_target="tpu_custom_call" | custom-call | flops 805306368 | bytes 12582912 | tf_op jit(solution)/shard_map/pallas_call | solution.py:80
  146.6 1.4 pad_maximum_fusion.1.send_ref
  148.0 6.3 %shard_map.57 = f32[112,64]{1,0:T(8,128)} custom-call(f32[112,64]{1,0:T(8,128)} %pad_maximum_fusion.1.send_ref), custom_call_target="tpu_custom_call" | custom-call | tf_op jit(solution)/shard_map/pallas_call | solution.py:269
  155.2 5.9 %cholesky.81 = f32[64,64]{1,0:T(8,128)S(1)} custom-call(f32[64,64]{1,0:T(8,128)S(1)} %copy.32), custom_call_target="Cholesky" | custom-call | tf_op jit(solution)/shard_map/jit(cholesky)/cholesky | solution.py:16
  162.4 4.9 %custom-call.19 = f32[1,64,64]{1,2,0:T(8,128)S(1)} custom-call(f32[1,64,64]{2,1,0:T(8,128)S(1)} %fusion.2), custom_call_target="InvertDiagBlocksLowerTriangular" | custom-call | tf_op jit(solution)/shard_map/triangular_solve | solution.py:18
  167.3 1.0 fusion.7
  169.4 9.9 %shard_map.58 = f32[64,1024]{1,0:T(8,128)} custom-call(f32[64,128]{1,0:T(8,128)} %copy-done, f32[64,768]{1,0:T(8,128)} %tile.21.tiled_ref, bf16[128,48,1024]{2,1,0:T(8,128)(2,1)} %slab_ref.7), custom_call_target="tpu_custom_call" | custom-call | flops 805306368 | bytes 12582912 | tf_op jit(solution)/shard_map/pallas_call | solution.py:126
  179.2 1.9 copy.34
  181.2 20.8 %shard_map.59 = f32[16,64]{1,0:T(8,128)} custom-call(f32[8,8,16,64]{3,2,1,0:T(8,128)} %bitcast.65), custom_call_target="tpu_custom_call" | custom-call | tf_op jit(solution)/shard_map/pallas_call | solution.py:269
  202.0 1.3 copy.41
  (43 shorter events, 11.5 us)
Async XLA Ops:
  0.6 31.5 %copy-start.3 = (bf16[64,16]{0,1:T(8,128)(2,1)S(1)}, bf16[64,16]{0,1:T(8,128)(2,1)}, u32[]{:S(2)}) copy-start(bf16[64,16]{0,1:T(8,128)(2,1)} %param.5) | copy-start | bytes 6148
  0.6 31.3 %copy-start.2 = (bf16[64,48]{0,1:T(8,128)(2,1)S(1)}, bf16[64,48]{0,1:T(8,128)(2,1)}, u32[]{:S(2)}) copy-start(bf16[64,48]{0,1:T(8,128)(2,1)} %param.6) | copy-start | bytes 18436
  74.6 13.5 %copy-start = (f32[64,128]{1,0:T(8,128)}, f32[64,128]{1,0:T(8,128)S(1)}, u32[]{:S(2)}) copy-start(f32[64,128]{1,0:T(8,128)S(1)} %fusion.14.frames_ref) | copy-start | bytes 98308
  135.2 11.1 %copy-start.1 = (bf16[8,8,16,64]{3,2,1,0:T(8,128)(2,1)S(1)}, bf16[8,8,16,64]{3,2,1,0:T(8,128)(2,1)}, u32[]{:S(2)}) copy-start(bf16[8,8,16,64]{3,2,1,0:T(8,128)(2,1)} %shard_map.55) | copy-start | bytes 393220

commit v4 on v3

--- a/solution.py
+++ b/solution.py
@@ -24,7 +24,7 @@
     return jnp.dot(factor, factor.T, preferred_element_type=jnp.float32)
 
 
-STREAM_FRAMES = 16
+STREAM_FRAMES = 32
 
 
 def _frame_kernel(block_t_ref, second_t_ref, slab_ref, out_ref):

time: 204 us -> 198 us (0.971)
  Pallas kernels: 147 us -> 139 us
    pallas_call x2, Pallas kernels: 19.7 us -> 15.9 us  [accumulate_pass(): pl.pallas_call(_accumulate_kernel, grid=(frame_count // STREAM_FRAMES,),...]
where the time goes in v4:
time: 198 us; the launch traced here: 197 us
  Pallas kernels  139 us (70%)
  other arithmetic  41.4 us (21%)
  local copies, waits for them, and re-layouts  11.2 us (6%)
  matrix products  4.12 us (2%)
    pallas_call x6, Pallas kernels, col_exchange(): pl.pallas_call(functools.partial(_exchange_kernel, n, rows, mode), out_sh...  108 us
    another operation x9, other arithmetic, ridge_solve(): jnp.linalg.cholesky(gram + ridge_weight * jnp.eye(order_size, dtype=jnp.f...  19.6 us
    another operation x6, other arithmetic, ridge_solve(): lax.linalg.triangular_solve(factor_low, middle, left_side=True, lower=Tru...  16.6 us
    pallas_call x2, Pallas kernels, accumulate_pass(): pl.pallas_call(_accumulate_kernel, grid=(frame_count // STREAM_FRAMES,),...  15.9 us
    pallas_call x1, Pallas kernels, second_pass(): pl.pallas_call(_second_kernel, grid=(frame_count // STREAM_FRAMES,), in_s...  7.66 us
    pallas_call x1, Pallas kernels, frame_pass(): pl.pallas_call(_frame_kernel, grid=(frame_count // STREAM_FRAMES,), in_sp...  7.64 us

profile of v4, /device:TPU:24, one launch (start us, length us, event | category | flops | bytes accessed | tf_op | source)
XLA Modules:
  0.0 196.8 jit_solution(13271515108979302605)
XLA Ops:
  0.7 20.4 %shard_map.50 = bf16[8,8,16,64]{3,2,1,0:T(8,128)(2,1)} custom-call(bf16[16,64]{1,0:T(8,128)(2,1)} %bitcast.79), custom_call_target="tpu_custom_call" | custom-call | tf_op jit(solution)/shard_map/pallas_call | solution.py:269
  21.1 1.3 convert_bitcast_fusion.second_t_ref
  22.4 7.6 %shard_map.51 = f32[128,64]{1,0:T(8,128)} custom-call(bf16[1024,64]{1,0:T(8,128)(2,1)} %bitcast.69, f32[48,64]{1,0:T(8,128)} %convert_bitcast_fusion.second_t_ref, bf16[128,48,1024]{2,1,0:T(8,128)(2,1)} %slab_ref.7), custom_call_target="tpu_custom_call" | custom-call | flops 805306368 | bytes 12582912 | tf_op jit(solution)/shard_map/pallas_call | solution.py:64
  30.5 1.5 pad_maximum_fusion
  31.9 26.9 %shard_map.52 = f32[8,8,4,64]{3,2,1,0:T(4,128)} custom-call(f32[8,8,4,64]{3,2,1,0:T(4,128)} %bitcast.74), custom_call_target="tpu_custom_call" | custom-call | tf_op jit(solution)/shard_map/pallas_call | solution.py:269
  60.2 5.9 %cholesky.59 = f32[64,64]{1,0:T(8,128)S(1)} custom-call(f32[64,64]{1,0:T(8,128)S(1)} %copy.24), custom_call_target="Cholesky" | custom-call | tf_op jit(solution)/shard_map/jit(cholesky)/cholesky | solution.py:16
  67.4 4.9 %custom-call.17 = f32[1,64,64]{1,2,0:T(8,128)S(1)} custom-call(f32[1,64,64]{2,1,0:T(8,128)S(1)} %fusion), custom_call_target="InvertDiagBlocksLowerTriangular" | custom-call | tf_op jit(solution)/shard_map/triangular_solve | solution.py:18
  73.1 5.9 %cholesky.70 = f32[64,64]{1,0:T(8,128)S(1)} custom-call(f32[64,64]{1,0:T(8,128)S(1)} %copy.26), custom_call_target="Cholesky" | custom-call | tf_op jit(solution)/shard_map/jit(cholesky)/cholesky | solution.py:16
  80.3 4.9 %custom-call.18 = f32[1,64,64]{1,2,0:T(8,128)S(1)} custom-call(f32[1,64,64]{2,1,0:T(8,128)S(1)} %fusion.1), custom_call_target="InvertDiagBlocksLowerTriangular" | custom-call | tf_op jit(solution)/shard_map/triangular_solve | solution.py:18
  85.4 1.4 tile.9.tiled_ref
  86.8 8.0 %shard_map.53 = f32[64,1024]{1,0:T(8,128)} custom-call(f32[64,128]{1,0:T(8,128)} %copy-done, f32[64,1536]{1,0:T(8,128)} %tile.9.tiled_ref, bf16[128,48,1024]{2,1,0:T(8,128)(2,1)} %slab_ref.7), custom_call_target="tpu_custom_call" | custom-call | flops 805306368 | bytes 12582912 | tf_op jit(solution)/shard_map/pallas_call | solution.py:126
  94.7 1.9 copy.28
  96.7 18.2 %shard_map.54 = f32[16,64]{1,0:T(8,128)} custom-call(f32[8,8,16,64]{3,2,1,0:T(8,128)} %bitcast.64), custom_call_target="tpu_custom_call" | custom-call | tf_op jit(solution)/shard_map/pallas_call | solution.py:269
  116.6 15.4 %shard_map.55 = bf16[8,8,16,64]{3,2,1,0:T(8,128)(2,1)} custom-call(bf16[16,64]{1,0:T(8,128)(2,1)} %convolution_convert_fusion.send_ref), custom_call_target="tpu_custom_call" | custom-call | tf_op jit(solution)/shard_map/pallas_call | solution.py:269
  132.0 1.5 copy.29
  133.5 7.7 %shard_map.56 = f32[48,64]{1,0:T(8,128)} custom-call(bf16[1024,64]{1,0:T(8,128)(2,1)} %bitcast.68, f32[128,64]{1,0:T(8,128)} %bitcast.76, bf16[128,48,1024]{2,1,0:T(8,128)(2,1)} %slab_ref.7), custom_call_target="tpu_custom_call" | custom-call | flops 805306368 | bytes 12582912 | tf_op jit(solution)/shard_map/pallas_call | solution.py:80
  141.4 1.4 pad_maximum_fusion.1.send_ref
  142.8 6.3 %shard_map.57 = f32[112,64]{1,0:T(8,128)} custom-call(f32[112,64]{1,0:T(8,128)} %pad_maximum_fusion.1.send_ref), custom_call_target="tpu_custom_call" | custom-call | tf_op jit(solution)/shard_map/pallas_call | solution.py:269
  150.0 5.9 %cholesky.81 = f32[64,64]{1,0:T(8,128)S(1)} custom-call(f32[64,64]{1,0:T(8,128)S(1)} %copy.32), custom_call_target="Cholesky" | custom-call | tf_op jit(solution)/shard_map/jit(cholesky)/cholesky | solution.py:16
  157.2 4.9 %custom-call.19 = f32[1,64,64]{1,2,0:T(8,128)S(1)} custom-call(f32[1,64,64]{2,1,0:T(8,128)S(1)} %fusion.2), custom_call_target="InvertDiagBlocksLowerTriangular" | custom-call | tf_op jit(solution)/shard_map/triangular_solve | solution.py:18
  163.3 1.4 tile.21.tiled_ref
  164.7 8.0 %shard_map.58 = f32[64,1024]{1,0:T(8,128)} custom-call(f32[64,128]{1,0:T(8,128)} %copy-done, f32[64,1536]{1,0:T(8,128)} %tile.21.tiled_ref, bf16[128,48,1024]{2,1,0:T(8,128)(2,1)} %slab_ref.7), custom_call_target="tpu_custom_call" | custom-call | flops 805306368 | bytes 12582912 | tf_op jit(solution)/shard_map/pallas_call | solution.py:126
  172.7 1.9 copy.34
  174.6 20.8 %shard_map.59 = f32[16,64]{1,0:T(8,128)} custom-call(f32[8,8,16,64]{3,2,1,0:T(8,128)} %bitcast.65), custom_call_target="tpu_custom_call" | custom-call | tf_op jit(solution)/shard_map/pallas_call | solution.py:269
  (43 shorter events, 12.0 us)
Async XLA Ops:
  0.6 29.6 %copy-start.3 = (bf16[64,16]{0,1:T(8,128)(2,1)S(1)}, bf16[64,16]{0,1:T(8,128)(2,1)}, u32[]{:S(2)}) copy-start(bf16[64,16]{0,1:T(8,128)(2,1)} %param.5) | copy-start | bytes 6148
  0.6 29.4 %copy-start.2 = (bf16[64,48]{0,1:T(8,128)(2,1)S(1)}, bf16[64,48]{0,1:T(8,128)(2,1)}, u32[]{:S(2)}) copy-start(bf16[64,48]{0,1:T(8,128)(2,1)} %param.6) | copy-start | bytes 18436
  72.7 14.1 %copy-start = (f32[64,128]{1,0:T(8,128)}, f32[64,128]{1,0:T(8,128)S(1)}, u32[]{:S(2)}) copy-start(f32[64,128]{1,0:T(8,128)S(1)} %fusion.14.frames_ref) | copy-start | bytes 98308
  132.0 9.2 %copy-start.1 = (bf16[8,8,16,64]{3,2,1,0:T(8,128)(2,1)S(1)}, bf16[8,8,16,64]{3,2,1,0:T(8,128)(2,1)}, u32[]{:S(2)}) copy-start(bf16[8,8,16,64]{3,2,1,0:T(8,128)(2,1)} %shard_map.55) | copy-start | bytes 393220

commit v5 on v4

--- a/solution.py
+++ b/solution.py
@@ -226,16 +226,20 @@
     landing, s1, r1, partial = take(4)
     exchange(outer, high, in_high, lambda peer: send_ref.at[peer], landing, s1, r1)
     partial[...] = jnp.sum(landing[...], axis=0)
-    landing2, s2, r2 = take(3)
-    exchange(inner, low, in_low, lambda peer: partial.at[peer], landing2, s2, r2)
     if mode == "scatter":
+        landing2, s2, r2 = take(3)
+        exchange(inner, low, in_low, lambda peer: partial.at[peer], landing2, s2, r2)
         out_ref[...] = jnp.sum(landing2[...], axis=0)
         return
-    chunk, row_landing, s3, r3, total = take(5)
-    chunk[...] = jnp.sum(landing2[...], axis=0)
-    exchange(rows, row, in_row, lambda peer: chunk, row_landing, s3, r3)
+    landing2, s2, r2, bundle = take(4)
+    exchange(inner, low, in_low, lambda peer: partial, landing2, s2, r2)
+    bundle[...] = jnp.sum(landing2[...], axis=0)
+    row_landing, s3, r3, total = take(4)
+    exchange(rows, row, in_row, lambda peer: bundle, row_landing, s3, r3)
     total[...] = jnp.sum(row_landing[...], axis=0)
-    gather(total)
+    everything, s4, r4 = take(3)
+    exchange(outer, high, in_high, lambda peer: total, everything, s4, r4)
+    out_ref[...] = everything[...]
 
 
 def col_exchange(send, n, mode, collective_id):
@@ -261,11 +265,14 @@
     else:
         piece = tuple(send.shape[2:])
         out_shape = piece if mode == "scatter" else (outer, inner) + piece
-        scratch = stage(outer, (inner,) + piece) + [pltpu.VMEM((inner,) + piece, dtype)]
-        scratch += stage(inner, piece)
-        if mode == "allreduce":
-            scratch += [pltpu.VMEM(piece, dtype)] + stage(rows, piece) + [pltpu.VMEM(piece, dtype)]
-            scratch += stage(inner, piece) + stage(outer, (inner,) + piece)
+        bundle = (inner,) + piece
+        scratch = stage(outer, bundle) + [pltpu.VMEM(bundle, dtype)]
+        if mode == "scatter":
+            scratch += stage(inner, piece)
+        else:
+            scratch += stage(inner, bundle) + [pltpu.VMEM(bundle, dtype)]
+            scratch += stage(rows, bundle) + [pltpu.VMEM(bundle, dtype)]
+            scratch += stage(outer, bundle)
     return pl.pallas_call(
         functools.partial(_exchange_kernel, n, rows, mode),
         out_shape=jax.ShapeDtypeStruct(out_shape, dtype),

time: 198 us -> 195 us (0.985)
  Pallas kernels: 139 us -> 135 us
    pallas_call x6, Pallas kernels: 108 us -> 104 us  [col_exchange(): pl.pallas_call(functools.partial(_exchange_kernel, n, rows, mode), out_sh...]
where the time goes in v5:
time: 195 us; the launch traced here: 193 us
  Pallas kernels  135 us (69%)
  other arithmetic  41.4 us (21%)
  local copies, waits for them, and re-layouts  11.2 us (6%)
  matrix products  4.12 us (2%)
    pallas_call x6, Pallas kernels, col_exchange(): pl.pallas_call(functools.partial(_exchange_kernel, n, rows, mode), out_sh...  104 us
    another operation x9, other arithmetic, ridge_solve(): jnp.linalg.cholesky(gram + ridge_weight * jnp.eye(order_size, dtype=jnp.f...  19.6 us
    another operation x6, other arithmetic, ridge_solve(): lax.linalg.triangular_solve(factor_low, middle, left_side=True, lower=Tru...  16.6 us
    pallas_call x2, Pallas kernels, accumulate_pass(): pl.pallas_call(_accumulate_kernel, grid=(frame_count // STREAM_FRAMES,),...  15.9 us
    pallas_call x1, Pallas kernels, second_pass(): pl.pallas_call(_second_kernel, grid=(frame_count // STREAM_FRAMES,), in_s...  7.67 us
    pallas_call x1, Pallas kernels, frame_pass(): pl.pallas_call(_frame_kernel, grid=(frame_count // STREAM_FRAMES,), in_sp...  7.64 us

profile of v5, /device:TPU:24, one launch (start us, length us, event | category | flops | bytes accessed | tf_op | source)
XLA Modules:
  0.0 192.5 jit_solution(1608485576450246576)
XLA Ops:
  0.7 20.4 %shard_map.50 = bf16[8,8,16,64]{3,2,1,0:T(8,128)(2,1)} custom-call(bf16[16,64]{1,0:T(8,128)(2,1)} %bitcast.79), custom_call_target="tpu_custom_call" | custom-call | tf_op jit(solution)/shard_map/pallas_call | solution.py:276
  21.1 1.3 convert_bitcast_fusion.second_t_ref
  22.4 7.6 %shard_map.51 = f32[128,64]{1,0:T(8,128)} custom-call(bf16[1024,64]{1,0:T(8,128)(2,1)} %bitcast.69, f32[48,64]{1,0:T(8,128)} %convert_bitcast_fusion.second_t_ref, bf16[128,48,1024]{2,1,0:T(8,128)(2,1)} %slab_ref.7), custom_call_target="tpu_custom_call" | custom-call | flops 805306368 | bytes 12582912 | tf_op jit(solution)/shard_map/pallas_call | solution.py:64
  30.5 1.5 pad_maximum_fusion
  31.9 24.3 %shard_map.52 = f32[8,8,4,64]{3,2,1,0:T(4,128)} custom-call(f32[8,8,4,64]{3,2,1,0:T(4,128)} %bitcast.74), custom_call_target="tpu_custom_call" | custom-call | tf_op jit(solution)/shard_map/pallas_call | solution.py:276
  57.5 5.9 %cholesky.59 = f32[64,64]{1,0:T(8,128)S(1)} custom-call(f32[64,64]{1,0:T(8,128)S(1)} %copy.24), custom_call_target="Cholesky" | custom-call | tf_op jit(solution)/shard_map/jit(cholesky)/cholesky | solution.py:16
  64.7 4.9 %custom-call.17 = f32[1,64,64]{1,2,0:T(8,128)S(1)} custom-call(f32[1,64,64]{2,1,0:T(8,128)S(1)} %fusion), custom_call_target="InvertDiagBlocksLowerTriangular" | custom-call | tf_op jit(solution)/shard_map/triangular_solve | solution.py:18
  70.4 5.9 %cholesky.70 = f32[64,64]{1,0:T(8,128)S(1)} custom-call(f32[64,64]{1,0:T(8,128)S(1)} %copy.26), custom_call_target="Cholesky" | custom-call | tf_op jit(solution)/shard_map/jit(cholesky)/cholesky | solution.py:16
  77.6 4.9 %custom-call.18 = f32[1,64,64]{1,2,0:T(8,128)S(1)} custom-call(f32[1,64,64]{2,1,0:T(8,128)S(1)} %fusion.1), custom_call_target="InvertDiagBlocksLowerTriangular" | custom-call | tf_op jit(solution)/shard_map/triangular_solve | solution.py:18
  82.7 1.4 tile.9.tiled_ref
  84.1 8.0 %shard_map.53 = f32[64,1024]{1,0:T(8,128)} custom-call(f32[64,128]{1,0:T(8,128)} %copy-done, f32[64,1536]{1,0:T(8,128)} %tile.9.tiled_ref, bf16[128,48,1024]{2,1,0:T(8,128)(2,1)} %slab_ref.7), custom_call_target="tpu_custom_call" | custom-call | flops 805306368 | bytes 12582912 | tf_op jit(solution)/shard_map/pallas_call | solution.py:126
  92.1 1.9 %copy.28 = f32[1024,64]{1,0:T(8,128)} copy(f32[1024,64]{0,1:T(8,128)} %bitcast.66) | data formatting | bytes 524288 | tf_op jit(solution)/shard_map/transpose | solution.py:302
  94.0 17.8 %shard_map.54 = f32[16,64]{1,0:T(8,128)} custom-call(f32[8,8,16,64]{3,2,1,0:T(8,128)} %bitcast.64), custom_call_target="tpu_custom_call" | custom-call | tf_op jit(solution)/shard_map/pallas_call | solution.py:276
  113.6 16.3 %shard_map.55 = bf16[8,8,16,64]{3,2,1,0:T(8,128)(2,1)} custom-call(bf16[16,64]{1,0:T(8,128)(2,1)} %convolution_convert_fusion.send_ref), custom_call_target="tpu_custom_call" | custom-call | tf_op jit(solution)/shard_map/pallas_call | solution.py:276
  129.9 1.5 copy.29
  131.5 7.7 %shard_map.56 = f32[48,64]{1,0:T(8,128)} custom-call(bf16[1024,64]{1,0:T(8,128)(2,1)} %bitcast.68, f32[128,64]{1,0:T(8,128)} %bitcast.76, bf16[128,48,1024]{2,1,0:T(8,128)(2,1)} %slab_ref.7), custom_call_target="tpu_custom_call" | custom-call | flops 805306368 | bytes 12582912 | tf_op jit(solution)/shard_map/pallas_call | solution.py:80
  139.4 1.4 pad_maximum_fusion.1.send_ref
  140.7 6.3 %shard_map.57 = f32[112,64]{1,0:T(8,128)} custom-call(f32[112,64]{1,0:T(8,128)} %pad_maximum_fusion.1.send_ref), custom_call_target="tpu_custom_call" | custom-call | tf_op jit(solution)/shard_map/pallas_call | solution.py:276
  147.9 5.9 %cholesky.81 = f32[64,64]{1,0:T(8,128)S(1)} custom-call(f32[64,64]{1,0:T(8,128)S(1)} %copy.32), custom_call_target="Cholesky" | custom-call | tf_op jit(solution)/shard_map/jit(cholesky)/cholesky | solution.py:16
  155.1 4.9 %custom-call.19 = f32[1,64,64]{1,2,0:T(8,128)S(1)} custom-call(f32[1,64,64]{2,1,0:T(8,128)S(1)} %fusion.2), custom_call_target="InvertDiagBlocksLowerTriangular" | custom-call | tf_op jit(solution)/shard_map/triangular_solve | solution.py:18
  161.3 1.4 tile.21.tiled_ref
  162.7 8.0 %shard_map.58 = f32[64,1024]{1,0:T(8,128)} custom-call(f32[64,128]{1,0:T(8,128)} %copy-done, f32[64,1536]{1,0:T(8,128)} %tile.21.tiled_ref, bf16[128,48,1024]{2,1,0:T(8,128)(2,1)} %slab_ref.7), custom_call_target="tpu_custom_call" | custom-call | flops 805306368 | bytes 12582912 | tf_op jit(solution)/shard_map/pallas_call | solution.py:126
  170.6 1.9 %copy.34 = f32[1024,64]{1,0:T(8,128)} copy(f32[1024,64]{0,1:T(8,128)} %bitcast.67) | data formatting | bytes 524288 | tf_op jit(solution)/shard_map/transpose | solution.py:302
  172.6 18.6 %shard_map.59 = f32[16,64]{1,0:T(8,128)} custom-call(f32[8,8,16,64]{3,2,1,0:T(8,128)} %bitcast.65), custom_call_target="tpu_custom_call" | custom-call | tf_op jit(solution)/shard_map/pallas_call | solution.py:276
  (43 shorter events, 12.0 us)
Async XLA Ops:
  0.6 29.6 %copy-start.3 = (bf16[64,16]{0,1:T(8,128)(2,1)S(1)}, bf16[64,16]{0,1:T(8,128)(2,1)}, u32[]{:S(2)}) copy-start(bf16[64,16]{0,1:T(8,128)(2,1)} %param.5) | copy-start | bytes 6148
  0.6 29.4 %copy-start.2 = (bf16[64,48]{0,1:T(8,128)(2,1)S(1)}, bf16[64,48]{0,1:T(8,128)(2,1)}, u32[]{:S(2)}) copy-start(bf16[64,48]{0,1:T(8,128)(2,1)} %param.6) | copy-start | bytes 18436
  70.1 14.1 %copy-start = (f32[64,128]{1,0:T(8,128)}, f32[64,128]{1,0:T(8,128)S(1)}, u32[]{:S(2)}) copy-start(f32[64,128]{1,0:T(8,128)S(1)} %fusion.14.frames_ref) | copy-start | bytes 98308
  129.9 9.2 %copy-start.1 = (bf16[8,8,16,64]{3,2,1,0:T(8,128)(2,1)S(1)}, bf16[8,8,16,64]{3,2,1,0:T(8,128)(2,1)}, u32[]{:S(2)}) copy-start(bf16[8,8,16,64]{3,2,1,0:T(8,128)(2,1)} %shard_map.55) | copy-start | bytes 393220

commit v6 on v5

--- a/solution.py
+++ b/solution.py
@@ -141,7 +141,13 @@
     return inner, n // inner
 
 
-def _exchange_kernel(n, rows, mode, send_ref, out_ref, *scratch):
+def _exchange_kernel(n, rows, mode, *refs):
+    if mode == "solve":
+        send_ref, op_ref, out_ref = refs[:3]
+        scratch = refs[3:]
+    else:
+        send_ref, out_ref = refs[:2]
+        scratch = refs[2:]
     me = lax.axis_index("col")
     row = lax.axis_index("row")
     inner, outer = _split(n)
@@ -231,6 +237,15 @@
         exchange(inner, low, in_low, lambda peer: partial.at[peer], landing2, s2, r2)
         out_ref[...] = jnp.sum(landing2[...], axis=0)
         return
+    if mode == "solve":
+        landing2, s2, r2, solved = take(4)
+        exchange(inner, low, in_low, lambda peer: partial.at[peer], landing2, s2, r2)
+        chunk = jnp.sum(landing2[...], axis=0)
+        solved[...] = jnp.dot(
+            chunk, op_ref[...], precision=lax.Precision.HIGHEST, preferred_element_type=jnp.float32
+        ).astype(solved.dtype)
+        gather(solved)
+        return
     landing2, s2, r2, bundle = take(4)
     exchange(inner, low, in_low, lambda peer: partial, landing2, s2, r2)
     bundle[...] = jnp.sum(landing2[...], axis=0)
@@ -242,14 +257,14 @@
     out_ref[...] = everything[...]
 
 
-def col_exchange(send, n, mode, collective_id):
+def col_exchange(send, n, mode, collective_id, op=None, out_dtype=None):
     rows = lax.axis_size("row")
     inner, outer = _split(n)
     dtype = send.dtype
 
-    def stage(count, piece):
+    def stage(count, piece, kind=dtype):
         return [
-            pltpu.VMEM((count,) + piece, dtype),
+            pltpu.VMEM((count,) + piece, kind),
             pltpu.SemaphoreType.DMA((count,)),
             pltpu.SemaphoreType.DMA((count,)),
         ]
@@ -269,18 +284,23 @@
         scratch = stage(outer, bundle) + [pltpu.VMEM(bundle, dtype)]
         if mode == "scatter":
             scratch += stage(inner, piece)
+        elif mode == "solve":
+            out_shape = (outer, inner) + piece
+            scratch += stage(inner, piece) + [pltpu.VMEM(piece, out_dtype)]
+            scratch += stage(inner, piece, out_dtype) + stage(outer, (inner,) + piece, out_dtype)
         else:
             scratch += stage(inner, bundle) + [pltpu.VMEM(bundle, dtype)]
             scratch += stage(rows, bundle) + [pltpu.VMEM(bundle, dtype)]
             scratch += stage(outer, bundle)
+    operands = (send,) if op is None else (send, op)
     return pl.pallas_call(
         functools.partial(_exchange_kernel, n, rows, mode),
-        out_shape=jax.ShapeDtypeStruct(out_shape, dtype),
-        in_specs=[pl.BlockSpec(memory_space=pltpu.VMEM)],
+        out_shape=jax.ShapeDtypeStruct(out_shape, out_dtype or dtype),
+        in_specs=[pl.BlockSpec(memory_space=pltpu.VMEM)] * len(operands),
         out_specs=pl.BlockSpec(memory_space=pltpu.VMEM),
         scratch_shapes=scratch,
         compiler_params=pltpu.CompilerParams(collective_id=collective_id, has_side_effects=True),
-    )(send)
+    )(*operands)
 
 
 def _chunk_order(chunks, n):
@@ -308,6 +328,15 @@
     chunks = _chunk_order(full.T.reshape(n, width, full.shape[0]), n)
     summed_t = _col_order(col_exchange(chunks, n, "allreduce", collective_id), n)
     return summed_t.reshape(n * width, full.shape[0]).T
+
+
+def solve_and_gather_t(full, operator_t, n, collective_id):
+    width = full.shape[1] // n
+    chunks = _chunk_order(full.T.reshape(n, width, full.shape[0]), n)
+    gathered = col_exchange(
+        chunks, n, "solve", collective_id, op=operator_t, out_dtype=jnp.bfloat16
+    )
+    return gathered.reshape(n * width, full.shape[0])
 
 
 def row_sum(piece, n, collective_id):
@@ -331,9 +360,8 @@
     frames = ridge_solve(gram_first * gram_second, frame_sum)
     gram_frames = jnp.dot(frames, frames.T, precision=lax.Precision.HIGHEST)
     full_part = accumulate_pass(tensor, frames, second_values)
-    first_sum_mine = col_reduce_scatter(full_part, n, 1)
-    new_first_mine = ridge_solve(gram_second * gram_frames, first_sum_mine).astype(jnp.bfloat16)
-    new_block_t = col_gather_t(new_first_mine.T, n)
+    inverse = ridge_solve(gram_second * gram_frames, jnp.eye(components, dtype=jnp.float32))
+    new_block_t = solve_and_gather_t(full_part, inverse.T, n, 1)
     gram_new_part = lax.dot_general(
         new_block_t, new_block_t, (((0,), (0,)), ((), ())), preferred_element_type=jnp.float32
     )

time: 195 us -> 190 us (0.974)
  Pallas kernels: 135 us -> 132 us
    pallas_call x6 -> x5, Pallas kernels: 104 us -> 101 us  [col_exchange(): pl.pallas_call(functools.partial(_exchange_kernel, n, rows, mode), out_sh...]
where the time goes in v6:
time: 190 us; the launch traced here: 189 us
  Pallas kernels  132 us (69%)
  other arithmetic  41.4 us (22%)
  local copies, waits for them, and re-layouts  11.2 us (6%)
  matrix products  3.43 us (2%)
    pallas_call x5, Pallas kernels, col_exchange(): pl.pallas_call(functools.partial(_exchange_kernel, n, rows, mode), out_sh...  101 us
    another operation x9, other arithmetic, ridge_solve(): jnp.linalg.cholesky(gram + ridge_weight * jnp.eye(order_size, dtype=jnp.f...  19.6 us
    another operation x6, other arithmetic, ridge_solve(): lax.linalg.triangular_solve(factor_low, middle, left_side=True, lower=Tru...  16.6 us
    pallas_call x2, Pallas kernels, accumulate_pass(): pl.pallas_call(_accumulate_kernel, grid=(frame_count // STREAM_FRAMES,),...  15.9 us
    pallas_call x1, Pallas kernels, second_pass(): pl.pallas_call(_second_kernel, grid=(frame_count // STREAM_FRAMES,), in_s...  7.65 us
    pallas_call x1, Pallas kernels, frame_pass(): pl.pallas_call(_frame_kernel, grid=(frame_count // STREAM_FRAMES,), in_sp...  7.65 us

profile of v6, /device:TPU:24, one launch (start us, length us, event | category | flops | bytes accessed | tf_op | source)
XLA Modules:
  0.0 188.8 jit_solution(13886176803574983292)
XLA Ops:
  0.7 20.4 %shard_map.50 = bf16[8,8,16,64]{3,2,1,0:T(8,128)(2,1)} custom-call(bf16[16,64]{1,0:T(8,128)(2,1)} %bitcast.78), custom_call_target="tpu_custom_call" | custom-call | tf_op jit(solution)/shard_map/pallas_call | solution.py:296
  21.1 1.3 convert_bitcast_fusion.second_t_ref
  22.4 7.6 %shard_map.51 = f32[128,64]{1,0:T(8,128)} custom-call(bf16[1024,64]{1,0:T(8,128)(2,1)} %bitcast.68, f32[48,64]{1,0:T(8,128)} %convert_bitcast_fusion.second_t_ref, bf16[128,48,1024]{2,1,0:T(8,128)(2,1)} %slab_ref.7), custom_call_target="tpu_custom_call" | custom-call | flops 805306368 | bytes 12582912 | tf_op jit(solution)/shard_map/pallas_call | solution.py:64
  30.5 1.5 pad_maximum_fusion
  32.0 24.3 %shard_map.52 = f32[8,8,4,64]{3,2,1,0:T(4,128)} custom-call(f32[8,8,4,64]{3,2,1,0:T(4,128)} %bitcast.73), custom_call_target="tpu_custom_call" | custom-call | tf_op jit(solution)/shard_map/pallas_call | solution.py:296
  57.6 5.9 %cholesky.59 = f32[64,64]{1,0:T(8,128)S(1)} custom-call(f32[64,64]{1,0:T(8,128)S(1)} %copy.24), custom_call_target="Cholesky" | custom-call | tf_op jit(solution)/shard_map/jit(cholesky)/cholesky | solution.py:16
  64.7 4.9 %custom-call.17 = f32[1,64,64]{1,2,0:T(8,128)S(1)} custom-call(f32[1,64,64]{2,1,0:T(8,128)S(1)} %fusion), custom_call_target="InvertDiagBlocksLowerTriangular" | custom-call | tf_op jit(solution)/shard_map/triangular_solve | solution.py:18
  70.4 5.9 %cholesky.70 = f32[64,64]{1,0:T(8,128)S(1)} custom-call(f32[64,64]{1,0:T(8,128)S(1)} %copy.28), custom_call_target="Cholesky" | custom-call | tf_op jit(solution)/shard_map/jit(cholesky)/cholesky | solution.py:16
  77.6 4.9 %custom-call.18 = f32[1,64,64]{1,2,0:T(8,128)S(1)} custom-call(f32[1,64,64]{2,1,0:T(8,128)S(1)} %fusion.1), custom_call_target="InvertDiagBlocksLowerTriangular" | custom-call | tf_op jit(solution)/shard_map/triangular_solve | solution.py:18
  83.8 1.4 tile.9.tiled_ref
  85.2 8.0 %shard_map.53 = f32[64,1024]{1,0:T(8,128)} custom-call(f32[64,128]{1,0:T(8,128)} %copy-done, f32[64,1536]{1,0:T(8,128)} %tile.9.tiled_ref, bf16[128,48,1024]{2,1,0:T(8,128)(2,1)} %slab_ref.7), custom_call_target="tpu_custom_call" | custom-call | flops 805306368 | bytes 12582912 | tf_op jit(solution)/shard_map/pallas_call | solution.py:126
  93.2 1.9 %copy.26 = f32[1024,64]{1,0:T(8,128)} copy(f32[1024,64]{0,1:T(8,128)} %bitcast.66) | data formatting | bytes 524288 | tf_op jit(solution)/shard_map/transpose | solution.py:335
  95.1 29.0 %shard_map.54 = bf16[8,8,16,64]{3,2,1,0:T(8,128)(2,1)} custom-call(f32[8,8,16,64]{3,2,1,0:T(8,128)} %bitcast.63, f32[64,64]{1,0:T(8,128)} %fusion.10.refs_1_), custom_call_target="tpu_custom_call" | custom-call | tf_op jit(solution)/shard_map/pallas_call | solution.py:296
  124.1 1.5 copy.29
  125.6 7.7 %shard_map.55 = f32[48,64]{1,0:T(8,128)} custom-call(bf16[1024,64]{1,0:T(8,128)(2,1)} %bitcast.65, f32[128,64]{1,0:T(8,128)} %bitcast.75, bf16[128,48,1024]{2,1,0:T(8,128)(2,1)} %slab_ref.7), custom_call_target="tpu_custom_call" | custom-call | flops 805306368 | bytes 12582912 | tf_op jit(solution)/shard_map/pallas_call | solution.py:80
  133.5 1.4 pad_maximum_fusion.1.refs_0_
  134.9 6.3 %shard_map.56 = f32[112,64]{1,0:T(8,128)} custom-call(f32[112,64]{1,0:T(8,128)} %pad_maximum_fusion.1.refs_0_), custom_call_target="tpu_custom_call" | custom-call | tf_op jit(solution)/shard_map/pallas_call | solution.py:296
  142.1 5.9 %cholesky.81 = f32[64,64]{1,0:T(8,128)S(1)} custom-call(f32[64,64]{1,0:T(8,128)S(1)} %copy.32), custom_call_target="Cholesky" | custom-call | tf_op jit(solution)/shard_map/jit(cholesky)/cholesky | solution.py:16
  149.3 4.9 %custom-call.19 = f32[1,64,64]{1,2,0:T(8,128)S(1)} custom-call(f32[1,64,64]{2,1,0:T(8,128)S(1)} %fusion.2), custom_call_target="InvertDiagBlocksLowerTriangular" | custom-call | tf_op jit(solution)/shard_map/triangular_solve | solution.py:18
  155.4 1.4 tile.21.tiled_ref
  156.8 8.0 %shard_map.57 = f32[64,1024]{1,0:T(8,128)} custom-call(f32[64,128]{1,0:T(8,128)} %copy-done, f32[64,1536]{1,0:T(8,128)} %tile.21.tiled_ref, bf16[128,48,1024]{2,1,0:T(8,128)(2,1)} %slab_ref.7), custom_call_target="tpu_custom_call" | custom-call | flops 805306368 | bytes 12582912 | tf_op jit(solution)/shard_map/pallas_call | solution.py:126
  164.8 1.9 %copy.34 = f32[1024,64]{1,0:T(8,128)} copy(f32[1024,64]{0,1:T(8,128)} %bitcast.67) | data formatting | bytes 524288 | tf_op jit(solution)/shard_map/transpose | solution.py:322
  166.8 20.7 %shard_map.58 = f32[16,64]{1,0:T(8,128)} custom-call(f32[8,8,16,64]{3,2,1,0:T(8,128)} %bitcast.64), custom_call_target="tpu_custom_call" | custom-call | tf_op jit(solution)/shard_map/pallas_call | solution.py:296
  187.5 1.3 copy.41
  (42 shorter events, 10.0 us)
Async XLA Ops:
  0.6 29.6 %copy-start.3 = (bf16[64,16]{0,1:T(8,128)(2,1)S(1)}, bf16[64,16]{0,1:T(8,128)(2,1)}, u32[]{:S(2)}) copy-start(bf16[64,16]{0,1:T(8,128)(2,1)} %param.5) | copy-start | bytes 6148
  0.6 29.4 %copy-start.2 = (bf16[64,48]{0,1:T(8,128)(2,1)S(1)}, bf16[64,48]{0,1:T(8,128)(2,1)}, u32[]{:S(2)}) copy-start(bf16[64,48]{0,1:T(8,128)(2,1)} %param.6) | copy-start | bytes 18436
  70.1 15.1 %copy-start = (f32[64,128]{1,0:T(8,128)}, f32[64,128]{1,0:T(8,128)S(1)}, u32[]{:S(2)}) copy-start(f32[64,128]{1,0:T(8,128)S(1)} %fusion.15.frames_ref) | copy-start | bytes 98308
  124.1 9.2 %copy-start.1 = (bf16[8,8,16,64]{3,2,1,0:T(8,128)(2,1)S(1)}, bf16[8,8,16,64]{3,2,1,0:T(8,128)(2,1)}, u32[]{:S(2)}) copy-start(bf16[8,8,16,64]{3,2,1,0:T(8,128)(2,1)} %shard_map.54) | copy-start | bytes 393220

commit v7 on v6

--- a/solution.py
+++ b/solution.py
@@ -94,13 +94,13 @@
     )(block_t, frames_t, tensor)
 
 
-def _accumulate_kernel(frames_ref, tiled_ref, slab_ref, out_ref):
+def _accumulate_kernel(frames_ref, tiled_ref, slab_ref, out_ref, total_ref):
     frames, width, rows = slab_ref.shape
     step = pl.program_id(0)
 
     @pl.when(step == 0)
     def _():
-        out_ref[...] = jnp.zeros_like(out_ref)
+        total_ref[...] = jnp.zeros_like(total_ref)
 
     frame_count = frames_ref.shape[1]
     span = frames * width
@@ -114,12 +114,16 @@
         rest = rest - piece.astype(jnp.float32)
         repeated = repeated + jnp.dot(piece, expand, preferred_element_type=jnp.float32)
     weights = (repeated * tiled_ref[...]).astype(jnp.bfloat16)
-    out_ref[...] += jnp.dot(
+    total_ref[...] += jnp.dot(
         weights, slab_ref[...].reshape(span, rows), preferred_element_type=jnp.float32
     )
 
-
-def accumulate_pass(tensor, frames, second):
+    @pl.when(step == pl.num_programs(0) - 1)
+    def _():
+        out_ref[...] = total_ref[...].T
+
+
+def accumulate_pass_t(tensor, frames, second):
     frame_count, width, rows = tensor.shape
     components = frames.shape[0]
     tiled = jnp.tile(second, (1, STREAM_FRAMES))
@@ -127,8 +131,9 @@
         _accumulate_kernel,
         grid=(frame_count // STREAM_FRAMES,),
         in_specs=[_whole(frames.shape), _whole(tiled.shape), _slab_spec(width, rows)],
-        out_specs=_whole((components, rows)),
-        out_shape=jax.ShapeDtypeStruct((components, rows), jnp.float32),
+        out_specs=_whole((rows, components)),
+        out_shape=jax.ShapeDtypeStruct((rows, components), jnp.float32),
+        scratch_shapes=[pltpu.VMEM((components, rows), jnp.float32)],
         cost_estimate=pl.CostEstimate(
             flops=2 * components * frame_count * width * rows, transcendentals=0,
             bytes_accessed=2 * frame_count * width * rows,
@@ -317,9 +322,9 @@
     return gathered.reshape(n * piece_t.shape[0], piece_t.shape[1])
 
 
-def col_reduce_scatter(full, n, collective_id):
-    width = full.shape[1] // n
-    chunks = _chunk_order(full.T.reshape(n, width, full.shape[0]), n)
+def col_reduce_scatter(full_t, n, collective_id):
+    width = full_t.shape[0] // n
+    chunks = _chunk_order(full_t.reshape(n, width, full_t.shape[1]), n)
     return col_exchange(chunks, n, "scatter", collective_id).T
 
 
@@ -330,13 +335,13 @@
     return summed_t.reshape(n * width, full.shape[0]).T
 
 
-def solve_and_gather_t(full, operator_t, n, collective_id):
-    width = full.shape[1] // n
-    chunks = _chunk_order(full.T.reshape(n, width, full.shape[0]), n)
+def solve_and_gather_t(full_t, operator_t, n, collective_id):
+    width = full_t.shape[0] // n
+    chunks = _chunk_order(full_t.reshape(n, width, full_t.shape[1]), n)
     gathered = col_exchange(
         chunks, n, "solve", collective_id, op=operator_t, out_dtype=jnp.bfloat16
     )
-    return gathered.reshape(n * width, full.shape[0])
+    return gathered.reshape(n * width, full_t.shape[1])
 
 
 def row_sum(piece, n, collective_id):
@@ -359,7 +364,7 @@
     gram_second = summed[:, frame_count + components:]
     frames = ridge_solve(gram_first * gram_second, frame_sum)
     gram_frames = jnp.dot(frames, frames.T, precision=lax.Precision.HIGHEST)
-    full_part = accumulate_pass(tensor, frames, second_values)
+    full_part = accumulate_pass_t(tensor, frames, second_values)
     inverse = ridge_solve(gram_second * gram_frames, jnp.eye(components, dtype=jnp.float32))
     new_block_t = solve_and_gather_t(full_part, inverse.T, n, 1)
     gram_new_part = lax.dot_general(
@@ -370,7 +375,7 @@
     second_sum = summed_new[:col_count].T
     gram_new = summed_new[col_count:]
     new_second = ridge_solve(gram_new * gram_frames, second_sum)
-    full_next = accumulate_pass(tensor, frames, new_second)
+    full_next = accumulate_pass_t(tensor, frames, new_second)
     mode_one = col_reduce_scatter(full_next, n, 2)
     return (frames, mode_one)
 

time: 190 us -> 186 us (0.979)
  local copies, waits for them, and re-layouts: 11.2 us -> 7.34 us
    transpose x2 -> x0, local copies, waits for them, and re-layouts: 3.89 us -> none  [the longest x1 1.94 us: solve_and_gather_t(): chunks = _chunk_order(full.T.reshape(n, width, full.shape[0]), n)]
where the time goes in v7:
time: 186 us; the launch traced here: 185 us
  Pallas kernels  132 us (71%)
  other arithmetic  41.4 us (22%)
  local copies, waits for them, and re-layouts  7.34 us (4%)
  matrix products  3.44 us (2%)
    pallas_call x5, Pallas kernels, col_exchange(): pl.pallas_call(functools.partial(_exchange_kernel, n, rows, mode), out_sh...  101 us
    another operation x9, other arithmetic, ridge_solve(): jnp.linalg.cholesky(gram + ridge_weight * jnp.eye(order_size, dtype=jnp.f...  19.6 us
    another operation x6, other arithmetic, ridge_solve(): lax.linalg.triangular_solve(factor_low, middle, left_side=True, lower=Tru...  16.6 us
    pallas_call x2, Pallas kernels, accumulate_pass_t(): pl.pallas_call(_accumulate_kernel, grid=(frame_count // STREAM_FRAMES,),...  16.5 us
    pallas_call x1, Pallas kernels, second_pass(): pl.pallas_call(_second_kernel, grid=(frame_count // STREAM_FRAMES,), in_s...  7.65 us
    pallas_call x1, Pallas kernels, frame_pass(): pl.pallas_call(_frame_kernel, grid=(frame_count // STREAM_FRAMES,), in_sp...  7.65 us

profile of v7, /device:TPU:24, one launch (start us, length us, event | category | flops | bytes accessed | tf_op | source)
XLA Modules:
  0.0 185.5 jit_solution(11491397862584706562)
XLA Ops:
  0.7 20.4 %shard_map.50 = bf16[8,8,16,64]{3,2,1,0:T(8,128)(2,1)} custom-call(bf16[16,64]{1,0:T(8,128)(2,1)} %bitcast.74), custom_call_target="tpu_custom_call" | custom-call | tf_op jit(solution)/shard_map/pallas_call | solution.py:301
  21.1 1.3 convert_bitcast_fusion.second_t_ref
  22.4 7.6 %shard_map.51 = f32[128,64]{1,0:T(8,128)} custom-call(bf16[1024,64]{1,0:T(8,128)(2,1)} %bitcast.64, f32[48,64]{1,0:T(8,128)} %convert_bitcast_fusion.second_t_ref, bf16[128,48,1024]{2,1,0:T(8,128)(2,1)} %slab_ref.7), custom_call_target="tpu_custom_call" | custom-call | flops 805306368 | bytes 12582912 | tf_op jit(solution)/shard_map/pallas_call | solution.py:64
  30.5 1.5 pad_maximum_fusion
  32.0 24.3 %shard_map.52 = f32[8,8,4,64]{3,2,1,0:T(4,128)} custom-call(f32[8,8,4,64]{3,2,1,0:T(4,128)} %bitcast.69), custom_call_target="tpu_custom_call" | custom-call | tf_op jit(solution)/shard_map/pallas_call | solution.py:301
  56.2 1.0 copy.20
  57.6 5.9 %cholesky.59 = f32[64,64]{1,0:T(8,128)S(1)} custom-call(f32[64,64]{1,0:T(8,128)S(1)} %copy.22), custom_call_target="Cholesky" | custom-call | tf_op jit(solution)/shard_map/jit(cholesky)/cholesky | solution.py:16
  64.7 4.9 %custom-call.17 = f32[1,64,64]{1,2,0:T(8,128)S(1)} custom-call(f32[1,64,64]{2,1,0:T(8,128)S(1)} %fusion), custom_call_target="InvertDiagBlocksLowerTriangular" | custom-call | tf_op jit(solution)/shard_map/triangular_solve | solution.py:18
  70.4 5.9 %cholesky.70 = f32[64,64]{1,0:T(8,128)S(1)} custom-call(f32[64,64]{1,0:T(8,128)S(1)} %copy.25), custom_call_target="Cholesky" | custom-call | tf_op jit(solution)/shard_map/jit(cholesky)/cholesky | solution.py:16
  77.6 4.9 %custom-call.18 = f32[1,64,64]{1,2,0:T(8,128)S(1)} custom-call(f32[1,64,64]{2,1,0:T(8,128)S(1)} %fusion.1), custom_call_target="InvertDiagBlocksLowerTriangular" | custom-call | tf_op jit(solution)/shard_map/triangular_solve | solution.py:18
  83.8 1.4 tile.9.tiled_ref
  85.2 8.3 %shard_map.53 = f32[1024,64]{1,0:T(8,128)} custom-call(f32[64,128]{1,0:T(8,128)} %copy-done, f32[64,1536]{1,0:T(8,128)} %tile.9.tiled_ref, bf16[128,48,1024]{2,1,0:T(8,128)(2,1)} %slab_ref.7), custom_call_target="tpu_custom_call" | custom-call | flops 805306368 | bytes 12582912 | tf_op jit(solution)/shard_map/pallas_call | solution.py:130
  93.5 29.0 %shard_map.54 = bf16[8,8,16,64]{3,2,1,0:T(8,128)(2,1)} custom-call(f32[8,8,16,64]{3,2,1,0:T(8,128)} %bitcast.61, f32[64,64]{1,0:T(8,128)} %fusion.10.refs_1_), custom_call_target="tpu_custom_call" | custom-call | tf_op jit(solution)/shard_map/pallas_call | solution.py:301
  122.5 1.5 copy.26
  124.0 7.7 %shard_map.55 = f32[48,64]{1,0:T(8,128)} custom-call(bf16[1024,64]{1,0:T(8,128)(2,1)} %bitcast.63, f32[128,64]{1,0:T(8,128)} %bitcast.71, bf16[128,48,1024]{2,1,0:T(8,128)(2,1)} %slab_ref.7), custom_call_target="tpu_custom_call" | custom-call | flops 805306368 | bytes 12582912 | tf_op jit(solution)/shard_map/pallas_call | solution.py:80
  131.9 1.4 pad_maximum_fusion.1.refs_0_
  133.3 6.3 %shard_map.56 = f32[112,64]{1,0:T(8,128)} custom-call(f32[112,64]{1,0:T(8,128)} %pad_maximum_fusion.1.refs_0_), custom_call_target="tpu_custom_call" | custom-call | tf_op jit(solution)/shard_map/pallas_call | solution.py:301
  140.5 5.9 %cholesky.81 = f32[64,64]{1,0:T(8,128)S(1)} custom-call(f32[64,64]{1,0:T(8,128)S(1)} %copy.29), custom_call_target="Cholesky" | custom-call | tf_op jit(solution)/shard_map/jit(cholesky)/cholesky | solution.py:16
  147.7 4.9 %custom-call.19 = f32[1,64,64]{1,2,0:T(8,128)S(1)} custom-call(f32[1,64,64]{2,1,0:T(8,128)S(1)} %fusion.2), custom_call_target="InvertDiagBlocksLowerTriangular" | custom-call | tf_op jit(solution)/shard_map/triangular_solve | solution.py:18
  152.5 1.0 fusion.7
  153.8 1.4 tile.21.tiled_ref
  155.2 8.3 %shard_map.57 = f32[1024,64]{1,0:T(8,128)} custom-call(f32[64,128]{1,0:T(8,128)} %copy-done, f32[64,1536]{1,0:T(8,128)} %tile.21.tiled_ref, bf16[128,48,1024]{2,1,0:T(8,128)(2,1)} %slab_ref.7), custom_call_target="tpu_custom_call" | custom-call | flops 805306368 | bytes 12582912 | tf_op jit(solution)/shard_map/pallas_call | solution.py:130
  163.5 20.7 %shard_map.58 = f32[16,64]{1,0:T(8,128)} custom-call(f32[8,8,16,64]{3,2,1,0:T(8,128)} %bitcast.62), custom_call_target="tpu_custom_call" | custom-call | tf_op jit(solution)/shard_map/pallas_call | solution.py:301
  184.2 1.3 copy.37
  (40 shorter events, 8.1 us)
Async XLA Ops:
  0.6 29.6 %copy-start.3 = (bf16[64,16]{0,1:T(8,128)(2,1)S(1)}, bf16[64,16]{0,1:T(8,128)(2,1)}, u32[]{:S(2)}) copy-start(bf16[64,16]{0,1:T(8,128)(2,1)} %param.5) | copy-start | bytes 6148
  0.6 29.4 %copy-start.2 = (bf16[64,48]{0,1:T(8,128)(2,1)S(1)}, bf16[64,48]{0,1:T(8,128)(2,1)}, u32[]{:S(2)}) copy-start(bf16[64,48]{0,1:T(8,128)(2,1)} %param.6) | copy-start | bytes 18436
  70.1 15.1 %copy-start = (f32[64,128]{1,0:T(8,128)}, f32[64,128]{1,0:T(8,128)S(1)}, u32[]{:S(2)}) copy-start(f32[64,128]{1,0:T(8,128)S(1)} %fusion.15.frames_ref) | copy-start | bytes 98308
  122.5 9.2 %copy-start.1 = (bf16[8,8,16,64]{3,2,1,0:T(8,128)(2,1)S(1)}, bf16[8,8,16,64]{3,2,1,0:T(8,128)(2,1)}, u32[]{:S(2)}) copy-start(bf16[8,8,16,64]{3,2,1,0:T(8,128)(2,1)} %shard_map.54) | copy-start | bytes 393220

commit v8 on v7

--- a/solution.py
+++ b/solution.py
@@ -1,6 +1,7 @@
 import functools
 
 import jax
+import numpy as np
 import jax.numpy as jnp
 from jax import lax
 from jax.experimental import pallas as pl
@@ -94,7 +95,7 @@
     )(block_t, frames_t, tensor)
 
 
-def _accumulate_kernel(frames_ref, tiled_ref, slab_ref, out_ref, total_ref):
+def _accumulate_kernel(frames_ref, second_ref, tile_ref, slab_ref, out_ref, total_ref):
     frames, width, rows = slab_ref.shape
     step = pl.program_id(0)
 
@@ -107,13 +108,18 @@
     which = lax.broadcasted_iota(jnp.int32, (frame_count, span), 0) - step * frames
     column = lax.broadcasted_iota(jnp.int32, (frame_count, span), 1)
     expand = ((column >= which * width) & (column < which * width + width)).astype(jnp.bfloat16)
-    rest = frames_ref[...]
-    repeated = jnp.zeros((frames_ref.shape[0], span), jnp.float32)
-    for _ in range(3):
-        piece = rest.astype(jnp.bfloat16)
-        rest = rest - piece.astype(jnp.float32)
-        repeated = repeated + jnp.dot(piece, expand, preferred_element_type=jnp.float32)
-    weights = (repeated * tiled_ref[...]).astype(jnp.bfloat16)
+    def spread(values, selector):
+        rest = values
+        repeated = jnp.zeros((values.shape[0], span), jnp.float32)
+        for _ in range(3):
+            piece = rest.astype(jnp.bfloat16)
+            rest = rest - piece.astype(jnp.float32)
+            repeated = repeated + jnp.dot(piece, selector, preferred_element_type=jnp.float32)
+        return repeated
+
+    weights = (spread(frames_ref[...], expand) * spread(second_ref[...], tile_ref[...])).astype(
+        jnp.bfloat16
+    )
     total_ref[...] += jnp.dot(
         weights, slab_ref[...].reshape(span, rows), preferred_element_type=jnp.float32
     )
@@ -126,11 +132,14 @@
 def accumulate_pass_t(tensor, frames, second):
     frame_count, width, rows = tensor.shape
     components = frames.shape[0]
-    tiled = jnp.tile(second, (1, STREAM_FRAMES))
+    tiler = jnp.asarray(np.tile(np.eye(width, dtype=np.float32), (1, STREAM_FRAMES)), jnp.bfloat16)
     return pl.pallas_call(
         _accumulate_kernel,
         grid=(frame_count // STREAM_FRAMES,),
-        in_specs=[_whole(frames.shape), _whole(tiled.shape), _slab_spec(width, rows)],
+        in_specs=[
+            _whole(frames.shape), _whole(second.shape), _whole(tiler.shape),
+            _slab_spec(width, rows),
+        ],
         out_specs=_whole((rows, components)),
         out_shape=jax.ShapeDtypeStruct((rows, components), jnp.float32),
         scratch_shapes=[pltpu.VMEM((components, rows), jnp.float32)],
@@ -138,7 +147,7 @@
             flops=2 * components * frame_count * width * rows, transcendentals=0,
             bytes_accessed=2 * frame_count * width * rows,
         ),
-    )(frames, tiled, tensor)
+    )(frames, second, tiler, tensor)
 
 
 def _split(n):

time: 186 us -> 188 us (1.011)
  matrix products: 3.44 us -> 6.61 us
    another operation x4 -> x0, local copies, waits for them, and re-layouts: 2.99 us -> none  [accumulate_pass_t(): tiled = jnp.tile(second, (1, STREAM_FRAMES))]
where the time goes in v8:
time: 188 us; the launch traced here: 187 us
  Pallas kernels  133 us (71%)
  other arithmetic  40.7 us (22%)
  matrix products  6.61 us (4%)
  local copies, waits for them, and re-layouts  6.1 us (3%)
    pallas_call x5, Pallas kernels, col_exchange(): pl.pallas_call(functools.partial(_exchange_kernel, n, rows, mode), out_sh...  101 us
    another operation x9, other arithmetic, ridge_solve(): jnp.linalg.cholesky(gram + ridge_weight * jnp.eye(order_size, dtype=jnp.f...  19.6 us
    pallas_call x2, Pallas kernels, accumulate_pass_t(): pl.pallas_call(_accumulate_kernel, grid=(frame_count // STREAM_FRAMES,),...  17.2 us
    another operation x6, other arithmetic, ridge_solve(): lax.linalg.triangular_solve(factor_low, middle, left_side=True, lower=Tru...  16.6 us
    pallas_call x1, Pallas kernels, second_pass(): pl.pallas_call(_second_kernel, grid=(frame_count // STREAM_FRAMES,), in_s...  7.65 us
    pallas_call x1, Pallas kernels, frame_pass(): pl.pallas_call(_frame_kernel, grid=(frame_count // STREAM_FRAMES,), in_sp...  7.64 us

profile of v8, /device:TPU:24, one launch (start us, length us, event | category | flops | bytes accessed | tf_op | source)
XLA Modules:
  0.0 187.2 jit_solution(1308670813336154295)
XLA Ops:
  0.6 1.0 convolution_multiply_fusion
  1.6 1.0 fusion.21
  2.6 20.3 %shard_map.68 = bf16[8,8,16,64]{3,2,1,0:T(8,128)(2,1)} custom-call(bf16[16,64]{1,0:T(8,128)(2,1)} %bitcast.74), custom_call_target="tpu_custom_call" | custom-call | tf_op jit(solution)/shard_map/pallas_call | solution.py:310
  25.0 7.6 %shard_map.69 = f32[128,64]{1,0:T(8,128)} custom-call(bf16[1024,64]{1,0:T(8,128)(2,1)} %bitcast.64, f32[48,64]{1,0:T(8,128)} %copy.22.second_t_ref, bf16[128,48,1024]{2,1,0:T(8,128)(2,1)} %slab_ref.7), custom_call_target="tpu_custom_call" | custom-call | flops 805306368 | bytes 12582912 | tf_op jit(solution)/shard_map/pallas_call | solution.py:65
  32.6 1.5 pad_maximum_fusion
  34.1 24.3 %shard_map.70 = f32[8,8,4,64]{3,2,1,0:T(4,128)} custom-call(f32[8,8,4,64]{3,2,1,0:T(4,128)} %bitcast.69), custom_call_target="tpu_custom_call" | custom-call | tf_op jit(solution)/shard_map/pallas_call | solution.py:310
  58.4 1.0 copy.25
  59.7 5.9 %cholesky.59 = f32[64,64]{1,0:T(8,128)S(1)} custom-call(f32[64,64]{1,0:T(8,128)S(1)} %copy.27), custom_call_target="Cholesky" | custom-call | tf_op jit(solution)/shard_map/jit(cholesky)/cholesky | solution.py:17
  66.9 4.9 %custom-call.17 = f32[1,64,64]{1,2,0:T(8,128)S(1)} custom-call(f32[1,64,64]{2,1,0:T(8,128)S(1)} %fusion), custom_call_target="InvertDiagBlocksLowerTriangular" | custom-call | tf_op jit(solution)/shard_map/triangular_solve | solution.py:19
  72.9 8.6 %shard_map.71 = f32[1024,64]{1,0:T(8,128)} custom-call(f32[64,128]{1,0:T(8,128)} %copy-done, f32[64,48]{1,0:T(8,128)} %get-tuple-element.3.second_ref, bf16[48,1536]{1,0:T(8,128)(2,1)} %constant.58.clone.tile_ref, bf16[128,48,1024]{2,1,0:T(8,128)(2,1)} %slab_ref.7), custom_call_target="tpu_custom_call" | custom-call | flops 805306368 | bytes 12582912 | tf_op jit(solution)/shard_map/pallas_call | solution.py:136
  81.6 5.9 %cholesky.70 = f32[64,64]{1,0:T(8,128)S(1)} custom-call(f32[64,64]{1,0:T(8,128)S(1)} %copy.29), custom_call_target="Cholesky" | custom-call | tf_op jit(solution)/shard_map/jit(cholesky)/cholesky | solution.py:17
  88.8 4.9 %custom-call.18 = f32[1,64,64]{1,2,0:T(8,128)S(1)} custom-call(f32[1,64,64]{2,1,0:T(8,128)S(1)} %fusion.1), custom_call_target="InvertDiagBlocksLowerTriangular" | custom-call | tf_op jit(solution)/shard_map/triangular_solve | solution.py:19
  94.8 29.0 %shard_map.72 = bf16[8,8,16,64]{3,2,1,0:T(8,128)(2,1)} custom-call(f32[8,8,16,64]{3,2,1,0:T(8,128)} %bitcast.61, f32[64,64]{1,0:T(8,128)} %fusion.10.refs_1_), custom_call_target="tpu_custom_call" | custom-call | tf_op jit(solution)/shard_map/pallas_call | solution.py:310
  123.8 1.3 convolution_bitcast_fusion
  125.0 1.5 copy.30
  126.5 7.7 %shard_map.73 = f32[48,64]{1,0:T(8,128)} custom-call(bf16[1024,64]{1,0:T(8,128)(2,1)} %bitcast.63, f32[128,64]{1,0:T(8,128)} %bitcast.71, bf16[128,48,1024]{2,1,0:T(8,128)(2,1)} %slab_ref.7), custom_call_target="tpu_custom_call" | custom-call | flops 805306368 | bytes 12582912 | tf_op jit(solution)/shard_map/pallas_call | solution.py:81
  134.2 1.4 pad_maximum_fusion.1.refs_0_
  135.5 6.3 %shard_map.74 = f32[112,64]{1,0:T(8,128)} custom-call(f32[112,64]{1,0:T(8,128)} %pad_maximum_fusion.1.refs_0_), custom_call_target="tpu_custom_call" | custom-call | tf_op jit(solution)/shard_map/pallas_call | solution.py:310
  142.7 5.9 %cholesky.81 = f32[64,64]{1,0:T(8,128)S(1)} custom-call(f32[64,64]{1,0:T(8,128)S(1)} %copy.33), custom_call_target="Cholesky" | custom-call | tf_op jit(solution)/shard_map/jit(cholesky)/cholesky | solution.py:17
  149.9 4.9 %custom-call.19 = f32[1,64,64]{1,2,0:T(8,128)S(1)} custom-call(f32[1,64,64]{2,1,0:T(8,128)S(1)} %fusion.2), custom_call_target="InvertDiagBlocksLowerTriangular" | custom-call | tf_op jit(solution)/shard_map/triangular_solve | solution.py:19
  154.8 1.0 fusion.7
  156.6 8.6 %shard_map.75 = f32[1024,64]{1,0:T(8,128)} custom-call(f32[64,128]{1,0:T(8,128)} %copy-done, f32[64,48]{1,0:T(8,128)} %fusion.5.second_ref, bf16[48,1536]{1,0:T(8,128)(2,1)} %constant.58.clone.tile_ref, bf16[128,48,1024]{2,1,0:T(8,128)(2,1)} %slab_ref.7), custom_call_target="tpu_custom_call" | custom-call | flops 805306368 | bytes 12582912 | tf_op jit(solution)/shard_map/pallas_call | solution.py:136
  165.2 20.7 %shard_map.76 = f32[16,64]{1,0:T(8,128)} custom-call(f32[8,8,16,64]{3,2,1,0:T(8,128)} %bitcast.62), custom_call_target="tpu_custom_call" | custom-call | tf_op jit(solution)/shard_map/pallas_call | solution.py:310
  185.9 1.3 copy.41
  (31 shorter events, 10.3 us)
Async XLA Ops:
  72.3 0.6 copy-start

commit v9 on v7

--- a/solution.py
+++ b/solution.py
@@ -25,6 +25,7 @@
 
 
 STREAM_FRAMES = 32
+PROJECT_FRAMES = 64
 
 
 def _frame_kernel(block_t_ref, second_t_ref, slab_ref, out_ref):
@@ -50,8 +51,8 @@
     out_ref[...] += jnp.sum(projected * frames_t_ref[...][:, None, :], axis=0)
 
 
-def _slab_spec(width, rows):
-    return pl.BlockSpec((STREAM_FRAMES, width, rows), lambda s: (s, 0, 0))
+def _slab_spec(width, rows, frames=STREAM_FRAMES):
+    return pl.BlockSpec((frames, width, rows), lambda s: (s, 0, 0))
 
 
 def _whole(shape):
@@ -63,9 +64,11 @@
     components = block_t.shape[1]
     return pl.pallas_call(
         _frame_kernel,
-        grid=(frame_count // STREAM_FRAMES,),
-        in_specs=[_whole(block_t.shape), _whole(second_t.shape), _slab_spec(width, rows)],
-        out_specs=pl.BlockSpec((STREAM_FRAMES, components), lambda s: (s, 0)),
+        grid=(frame_count // PROJECT_FRAMES,),
+        in_specs=[
+            _whole(block_t.shape), _whole(second_t.shape), _slab_spec(width, rows, PROJECT_FRAMES)
+        ],
+        out_specs=pl.BlockSpec((PROJECT_FRAMES, components), lambda s: (s, 0)),
         out_shape=jax.ShapeDtypeStruct((frame_count, components), jnp.float32),
         cost_estimate=pl.CostEstimate(
             flops=2 * components * frame_count * width * rows, transcendentals=0,
@@ -79,11 +82,11 @@
     components = block_t.shape[1]
     return pl.pallas_call(
         _second_kernel,
-        grid=(frame_count // STREAM_FRAMES,),
+        grid=(frame_count // PROJECT_FRAMES,),
         in_specs=[
             _whole(block_t.shape),
-            pl.BlockSpec((STREAM_FRAMES, components), lambda s: (s, 0)),
-            _slab_spec(width, rows),
+            pl.BlockSpec((PROJECT_FRAMES, components), lambda s: (s, 0)),
+            _slab_spec(width, rows, PROJECT_FRAMES),
         ],
         out_specs=_whole((width, components)),
         out_shape=jax.ShapeDtypeStruct((width, components), jnp.float32),

time: 186 us -> 185 us (level)
  no operation moved by 1% of the time
where the time goes in v9:
time: 185 us; the launch traced here: 184 us
  Pallas kernels  131 us (71%)
  other arithmetic  41.4 us (22%)
  local copies, waits for them, and re-layouts  7.34 us (4%)
  matrix products  3.44 us (2%)
    pallas_call x5, Pallas kernels, col_exchange(): pl.pallas_call(functools.partial(_exchange_kernel, n, rows, mode), out_sh...  101 us
    another operation x9, other arithmetic, ridge_solve(): jnp.linalg.cholesky(gram + ridge_weight * jnp.eye(order_size, dtype=jnp.f...  19.6 us
    another operation x6, other arithmetic, ridge_solve(): lax.linalg.triangular_solve(factor_low, middle, left_side=True, lower=Tru...  16.6 us
    pallas_call x2, Pallas kernels, accumulate_pass_t(): pl.pallas_call(_accumulate_kernel, grid=(frame_count // STREAM_FRAMES,),...  16.5 us
    pallas_call x1, Pallas kernels, second_pass(): pl.pallas_call(_second_kernel, grid=(frame_count // PROJECT_FRAMES,), in_...  7.12 us
    pallas_call x1, Pallas kernels, frame_pass(): pl.pallas_call(_frame_kernel, grid=(frame_count // PROJECT_FRAMES,), in_s...  7.11 us

profile of v9, /device:TPU:24, one launch (start us, length us, event | category | flops | bytes accessed | tf_op | source)
XLA Modules:
  0.0 184.4 jit_solution(12233818825453969074)
XLA Ops:
  0.7 20.4 %shard_map.50 = bf16[8,8,16,64]{3,2,1,0:T(8,128)(2,1)} custom-call(bf16[16,64]{1,0:T(8,128)(2,1)} %bitcast.74), custom_call_target="tpu_custom_call" | custom-call | tf_op jit(solution)/shard_map/pallas_call | solution.py:304
  21.1 1.3 convert_bitcast_fusion.second_t_ref
  22.4 7.1 %shard_map.51 = f32[128,64]{1,0:T(8,128)} custom-call(bf16[1024,64]{1,0:T(8,128)(2,1)} %bitcast.64, f32[48,64]{1,0:T(8,128)} %convert_bitcast_fusion.second_t_ref, bf16[128,48,1024]{2,1,0:T(8,128)(2,1)} %slab_ref.7), custom_call_target="tpu_custom_call" | custom-call | flops 805306368 | bytes 12582912 | tf_op jit(solution)/shard_map/pallas_call | solution.py:65
  29.9 1.5 pad_maximum_fusion
  31.4 24.3 %shard_map.52 = f32[8,8,4,64]{3,2,1,0:T(4,128)} custom-call(f32[8,8,4,64]{3,2,1,0:T(4,128)} %bitcast.69), custom_call_target="tpu_custom_call" | custom-call | tf_op jit(solution)/shard_map/pallas_call | solution.py:304
  55.7 1.0 copy.20
  57.0 5.9 %cholesky.59 = f32[64,64]{1,0:T(8,128)S(1)} custom-call(f32[64,64]{1,0:T(8,128)S(1)} %copy.22), custom_call_target="Cholesky" | custom-call | tf_op jit(solution)/shard_map/jit(cholesky)/cholesky | solution.py:16
  64.2 4.9 %custom-call.17 = f32[1,64,64]{1,2,0:T(8,128)S(1)} custom-call(f32[1,64,64]{2,1,0:T(8,128)S(1)} %fusion), custom_call_target="InvertDiagBlocksLowerTriangular" | custom-call | tf_op jit(solution)/shard_map/triangular_solve | solution.py:18
  69.9 5.9 %cholesky.70 = f32[64,64]{1,0:T(8,128)S(1)} custom-call(f32[64,64]{1,0:T(8,128)S(1)} %copy.25), custom_call_target="Cholesky" | custom-call | tf_op jit(solution)/shard_map/jit(cholesky)/cholesky | solution.py:16
  77.1 4.9 %custom-call.18 = f32[1,64,64]{1,2,0:T(8,128)S(1)} custom-call(f32[1,64,64]{2,1,0:T(8,128)S(1)} %fusion.1), custom_call_target="InvertDiagBlocksLowerTriangular" | custom-call | tf_op jit(solution)/shard_map/triangular_solve | solution.py:18
  83.2 1.4 tile.9.tiled_ref
  84.7 8.3 %shard_map.53 = f32[1024,64]{1,0:T(8,128)} custom-call(f32[64,128]{1,0:T(8,128)} %copy-done, f32[64,1536]{1,0:T(8,128)} %tile.9.tiled_ref, bf16[128,48,1024]{2,1,0:T(8,128)(2,1)} %slab_ref.7), custom_call_target="tpu_custom_call" | custom-call | flops 805306368 | bytes 12582912 | tf_op jit(solution)/shard_map/pallas_call | solution.py:133
  92.9 29.0 %shard_map.54 = bf16[8,8,16,64]{3,2,1,0:T(8,128)(2,1)} custom-call(f32[8,8,16,64]{3,2,1,0:T(8,128)} %bitcast.61, f32[64,64]{1,0:T(8,128)} %fusion.10.refs_1_), custom_call_target="tpu_custom_call" | custom-call | tf_op jit(solution)/shard_map/pallas_call | solution.py:304
  122.0 1.5 copy.26
  123.5 7.1 %shard_map.55 = f32[48,64]{1,0:T(8,128)} custom-call(bf16[1024,64]{1,0:T(8,128)(2,1)} %bitcast.63, f32[128,64]{1,0:T(8,128)} %bitcast.71, bf16[128,48,1024]{2,1,0:T(8,128)(2,1)} %slab_ref.7), custom_call_target="tpu_custom_call" | custom-call | flops 805306368 | bytes 12582912 | tf_op jit(solution)/shard_map/pallas_call | solution.py:83
  130.9 1.4 pad_maximum_fusion.1.refs_0_
  132.2 6.3 %shard_map.56 = f32[112,64]{1,0:T(8,128)} custom-call(f32[112,64]{1,0:T(8,128)} %pad_maximum_fusion.1.refs_0_), custom_call_target="tpu_custom_call" | custom-call | tf_op jit(solution)/shard_map/pallas_call | solution.py:304
  139.4 5.9 %cholesky.81 = f32[64,64]{1,0:T(8,128)S(1)} custom-call(f32[64,64]{1,0:T(8,128)S(1)} %copy.29), custom_call_target="Cholesky" | custom-call | tf_op jit(solution)/shard_map/jit(cholesky)/cholesky | solution.py:16
  146.6 4.9 %custom-call.19 = f32[1,64,64]{1,2,0:T(8,128)S(1)} custom-call(f32[1,64,64]{2,1,0:T(8,128)S(1)} %fusion.2), custom_call_target="InvertDiagBlocksLowerTriangular" | custom-call | tf_op jit(solution)/shard_map/triangular_solve | solution.py:18
  151.5 1.0 fusion.7
  152.8 1.4 tile.21.tiled_ref
  154.2 8.3 %shard_map.57 = f32[1024,64]{1,0:T(8,128)} custom-call(f32[64,128]{1,0:T(8,128)} %copy-done, f32[64,1536]{1,0:T(8,128)} %tile.21.tiled_ref, bf16[128,48,1024]{2,1,0:T(8,128)(2,1)} %slab_ref.7), custom_call_target="tpu_custom_call" | custom-call | flops 805306368 | bytes 12582912 | tf_op jit(solution)/shard_map/pallas_call | solution.py:133
  162.4 20.6 %shard_map.58 = f32[16,64]{1,0:T(8,128)} custom-call(f32[8,8,16,64]{3,2,1,0:T(8,128)} %bitcast.62), custom_call_target="tpu_custom_call" | custom-call | tf_op jit(solution)/shard_map/pallas_call | solution.py:304
  183.1 1.3 copy.37
  (40 shorter events, 8.1 us)
Async XLA Ops:
  0.6 29.1 %copy-start.3 = (bf16[64,16]{0,1:T(8,128)(2,1)S(1)}, bf16[64,16]{0,1:T(8,128)(2,1)}, u32[]{:S(2)}) copy-start(bf16[64,16]{0,1:T(8,128)(2,1)} %param.5) | copy-start | bytes 6148
  0.6 28.9 %copy-start.2 = (bf16[64,48]{0,1:T(8,128)(2,1)S(1)}, bf16[64,48]{0,1:T(8,128)(2,1)}, u32[]{:S(2)}) copy-start(bf16[64,48]{0,1:T(8,128)(2,1)} %param.6) | copy-start | bytes 18436
  69.5 15.1 %copy-start = (f32[64,128]{1,0:T(8,128)}, f32[64,128]{1,0:T(8,128)S(1)}, u32[]{:S(2)}) copy-start(f32[64,128]{1,0:T(8,128)S(1)} %fusion.15.frames_ref) | copy-start | bytes 98308
  122.0 8.7 %copy-start.1 = (bf16[8,8,16,64]{3,2,1,0:T(8,128)(2,1)S(1)}, bf16[8,8,16,64]{3,2,1,0:T(8,128)(2,1)}, u32[]{:S(2)}) copy-start(bf16[8,8,16,64]{3,2,1,0:T(8,128)(2,1)} %shard_map.54) | copy-start | bytes 393220

commit v10 on v9

--- a/solution.py
+++ b/solution.py
@@ -37,18 +37,21 @@
     out_ref[...] = jnp.sum(projected * second_t_ref[...][None], axis=1)
 
 
-def _second_kernel(block_t_ref, frames_t_ref, slab_ref, out_ref):
+def _second_kernel(block_t_ref, frames_ref, slab_ref, out_ref, frames_t_ref):
     frames, width, rows = slab_ref.shape
-
-    @pl.when(pl.program_id(0) == 0)
+    step = pl.program_id(0)
+
+    @pl.when(step == 0)
     def _():
         out_ref[...] = jnp.zeros_like(out_ref)
+        frames_t_ref[...] = frames_ref[...].T
 
     projected = jnp.dot(
         slab_ref[...].reshape(frames * width, rows), block_t_ref[...],
         preferred_element_type=jnp.float32,
     ).reshape(frames, width, block_t_ref.shape[1])
-    out_ref[...] += jnp.sum(projected * frames_t_ref[...][:, None, :], axis=0)
+    block_frames = frames_t_ref[pl.ds(pl.multiple_of(step * frames, frames), frames), :]
+    out_ref[...] += jnp.sum(projected * block_frames[:, None, :], axis=0)
 
 
 def _slab_spec(width, rows, frames=STREAM_FRAMES):
@@ -77,7 +80,7 @@
     )(block_t, second_t, tensor)
 
 
-def second_pass(tensor, block_t, frames_t):
+def second_pass(tensor, block_t, frames):
     frame_count, width, rows = tensor.shape
     components = block_t.shape[1]
     return pl.pallas_call(
@@ -85,16 +88,17 @@
         grid=(frame_count // PROJECT_FRAMES,),
         in_specs=[
             _whole(block_t.shape),
-            pl.BlockSpec((PROJECT_FRAMES, components), lambda s: (s, 0)),
+            _whole(frames.shape),
             _slab_spec(width, rows, PROJECT_FRAMES),
         ],
         out_specs=_whole((width, components)),
         out_shape=jax.ShapeDtypeStruct((width, components), jnp.float32),
+        scratch_shapes=[pltpu.VMEM((frame_count, components), jnp.float32)],
         cost_estimate=pl.CostEstimate(
             flops=2 * components * frame_count * width * rows, transcendentals=0,
             bytes_accessed=2 * frame_count * width * rows,
         ),
-    )(block_t, frames_t, tensor)
+    )(block_t, frames, tensor)
 
 
 def _accumulate_kernel(frames_ref, tiled_ref, slab_ref, out_ref, total_ref):
@@ -373,7 +377,7 @@
     gram_new_part = lax.dot_general(
         new_block_t, new_block_t, (((0,), (0,)), ((), ())), preferred_element_type=jnp.float32
     )
-    second_part_t = second_pass(tensor, new_block_t, frames.T)
+    second_part_t = second_pass(tensor, new_block_t, frames)
     summed_new = row_sum(jnp.concatenate([second_part_t, gram_new_part], axis=0), n, 4)
     second_sum = summed_new[:col_count].T
     gram_new = summed_new[col_count:]

time: 185 us -> 186 us (level)
  no operation moved by 1% of the time
where the time goes in v10:
time: 186 us; the launch traced here: 185 us
  Pallas kernels  131 us (70%)
  other arithmetic  41.4 us (22%)
  local copies, waits for them, and re-layouts  6.51 us (4%)
  matrix products  4.98 us (3%)
    pallas_call x5, Pallas kernels, col_exchange(): pl.pallas_call(functools.partial(_exchange_kernel, n, rows, mode), out_sh...  101 us
    another operation x9, other arithmetic, ridge_solve(): jnp.linalg.cholesky(gram + ridge_weight * jnp.eye(order_size, dtype=jnp.f...  19.6 us
    another operation x6, other arithmetic, ridge_solve(): lax.linalg.triangular_solve(factor_low, middle, left_side=True, lower=Tru...  16.6 us
    pallas_call x2, Pallas kernels, accumulate_pass_t(): pl.pallas_call(_accumulate_kernel, grid=(frame_count // STREAM_FRAMES,),...  16.5 us
    pallas_call x1, Pallas kernels, second_pass(): pl.pallas_call(_second_kernel, grid=(frame_count // PROJECT_FRAMES,), in_...  7.16 us
    pallas_call x1, Pallas kernels, frame_pass(): pl.pallas_call(_frame_kernel, grid=(frame_count // PROJECT_FRAMES,), in_s...  7.12 us

profile of v10, /device:TPU:24, one launch (start us, length us, event | category | flops | bytes accessed | tf_op | source)
XLA Modules:
  0.0 185.1 jit_solution(15475780827182783430)
XLA Ops:
  0.6 1.3 convert_bitcast_fusion.second_t_ref
  2.9 1.0 convolution_multiply_fusion
  4.7 20.4 %shard_map.50 = bf16[8,8,16,64]{3,2,1,0:T(8,128)(2,1)} custom-call(bf16[16,64]{1,0:T(8,128)(2,1)} %bitcast.72), custom_call_target="tpu_custom_call" | custom-call | tf_op jit(solution)/shard_map/pallas_call | solution.py:308
  25.1 7.1 %shard_map.51 = f32[128,64]{1,0:T(8,128)} custom-call(bf16[1024,64]{1,0:T(8,128)(2,1)} %bitcast.63, f32[48,64]{1,0:T(8,128)} %convert_bitcast_fusion.second_t_ref, bf16[128,48,1024]{2,1,0:T(8,128)(2,1)} %slab_ref.7), custom_call_target="tpu_custom_call" | custom-call | flops 805306368 | bytes 12582912 | tf_op jit(solution)/shard_map/pallas_call | solution.py:68
  32.2 1.5 pad_maximum_fusion
  33.7 24.3 %shard_map.52 = f32[8,8,4,64]{3,2,1,0:T(4,128)} custom-call(f32[8,8,4,64]{3,2,1,0:T(4,128)} %bitcast.68), custom_call_target="tpu_custom_call" | custom-call | tf_op jit(solution)/shard_map/pallas_call | solution.py:308
  58.0 1.0 copy.19
  59.3 5.9 %cholesky.59 = f32[64,64]{1,0:T(8,128)S(1)} custom-call(f32[64,64]{1,0:T(8,128)S(1)} %copy.21), custom_call_target="Cholesky" | custom-call | tf_op jit(solution)/shard_map/jit(cholesky)/cholesky | solution.py:16
  66.5 4.9 %custom-call.17 = f32[1,64,64]{1,2,0:T(8,128)S(1)} custom-call(f32[1,64,64]{2,1,0:T(8,128)S(1)} %fusion), custom_call_target="InvertDiagBlocksLowerTriangular" | custom-call | tf_op jit(solution)/shard_map/triangular_solve | solution.py:18
  72.2 5.9 %cholesky.70 = f32[64,64]{1,0:T(8,128)S(1)} custom-call(f32[64,64]{1,0:T(8,128)S(1)} %copy.24), custom_call_target="Cholesky" | custom-call | tf_op jit(solution)/shard_map/jit(cholesky)/cholesky | solution.py:16
  79.4 4.9 %custom-call.18 = f32[1,64,64]{1,2,0:T(8,128)S(1)} custom-call(f32[1,64,64]{2,1,0:T(8,128)S(1)} %fusion.1), custom_call_target="InvertDiagBlocksLowerTriangular" | custom-call | tf_op jit(solution)/shard_map/triangular_solve | solution.py:18
  85.4 1.4 tile.9.tiled_ref
  86.9 8.3 %shard_map.53 = f32[1024,64]{1,0:T(8,128)} custom-call(f32[64,128]{1,0:T(8,128)} %copy-done, f32[64,1536]{1,0:T(8,128)} %tile.9.tiled_ref, bf16[128,48,1024]{2,1,0:T(8,128)(2,1)} %slab_ref.7), custom_call_target="tpu_custom_call" | custom-call | flops 805306368 | bytes 12582912 | tf_op jit(solution)/shard_map/pallas_call | solution.py:137
  95.1 28.9 %shard_map.54 = bf16[8,8,16,64]{3,2,1,0:T(8,128)(2,1)} custom-call(f32[8,8,16,64]{3,2,1,0:T(8,128)} %bitcast.60, f32[64,64]{1,0:T(8,128)} %fusion.10.refs_1_), custom_call_target="tpu_custom_call" | custom-call | tf_op jit(solution)/shard_map/pallas_call | solution.py:308
  124.1 7.2 %shard_map.55 = f32[48,64]{1,0:T(8,128)} custom-call(bf16[1024,64]{1,0:T(8,128)(2,1)} %bitcast.62, f32[64,128]{1,0:T(8,128)} %copy-done, bf16[128,48,1024]{2,1,0:T(8,128)(2,1)} %slab_ref.7), custom_call_target="tpu_custom_call" | custom-call | flops 805306368 | bytes 12582912 | tf_op jit(solution)/shard_map/pallas_call | solution.py:86
  131.5 1.4 pad_maximum_fusion.1.refs_0_
  132.8 6.3 %shard_map.56 = f32[112,64]{1,0:T(8,128)} custom-call(f32[112,64]{1,0:T(8,128)} %pad_maximum_fusion.1.refs_0_), custom_call_target="tpu_custom_call" | custom-call | tf_op jit(solution)/shard_map/pallas_call | solution.py:308
  140.0 5.9 %cholesky.81 = f32[64,64]{1,0:T(8,128)S(1)} custom-call(f32[64,64]{1,0:T(8,128)S(1)} %copy.27), custom_call_target="Cholesky" | custom-call | tf_op jit(solution)/shard_map/jit(cholesky)/cholesky | solution.py:16
  147.2 4.9 %custom-call.19 = f32[1,64,64]{1,2,0:T(8,128)S(1)} custom-call(f32[1,64,64]{2,1,0:T(8,128)S(1)} %fusion.2), custom_call_target="InvertDiagBlocksLowerTriangular" | custom-call | tf_op jit(solution)/shard_map/triangular_solve | solution.py:18
  152.1 1.0 fusion.7
  153.4 1.4 tile.21.tiled_ref
  154.8 8.3 %shard_map.57 = f32[1024,64]{1,0:T(8,128)} custom-call(f32[64,128]{1,0:T(8,128)} %copy-done, f32[64,1536]{1,0:T(8,128)} %tile.21.tiled_ref, bf16[128,48,1024]{2,1,0:T(8,128)(2,1)} %slab_ref.7), custom_call_target="tpu_custom_call" | custom-call | flops 805306368 | bytes 12582912 | tf_op jit(solution)/shard_map/pallas_call | solution.py:137
  163.0 20.8 %shard_map.58 = f32[16,64]{1,0:T(8,128)} custom-call(f32[8,8,16,64]{3,2,1,0:T(8,128)} %bitcast.61), custom_call_target="tpu_custom_call" | custom-call | tf_op jit(solution)/shard_map/pallas_call | solution.py:308
  183.8 1.3 copy.35
  (35 shorter events, 9.3 us)
Async XLA Ops:
  71.8 15.0 %copy-start = (f32[64,128]{1,0:T(8,128)}, f32[64,128]{1,0:T(8,128)S(1)}, u32[]{:S(2)}) copy-start(f32[64,128]{1,0:T(8,128)S(1)} %fusion.15.frames_ref) | copy-start | bytes 98308
  124.0 7.2 %copy-start.1 = (bf16[8,8,16,64]{3,2,1,0:T(8,128)(2,1)S(1)}, bf16[8,8,16,64]{3,2,1,0:T(8,128)(2,1)}, u32[]{:S(2)}) copy-start(bf16[8,8,16,64]{3,2,1,0:T(8,128)(2,1)} %shard_map.54) | copy-start | bytes 393220

commit v11 on v9

--- a/solution.py
+++ b/solution.py
@@ -331,11 +331,11 @@
     return col_exchange(chunks, n, "scatter", collective_id).T
 
 
-def all_reduce(full, n, collective_id):
-    width = full.shape[1] // n
-    chunks = _chunk_order(full.T.reshape(n, width, full.shape[0]), n)
+def all_reduce_t(full_t, n, collective_id):
+    width = full_t.shape[0] // n
+    chunks = _chunk_order(full_t.reshape(n, width, full_t.shape[1]), n)
     summed_t = _col_order(col_exchange(chunks, n, "allreduce", collective_id), n)
-    return summed_t.reshape(n * width, full.shape[0]).T
+    return summed_t.reshape(full_t.shape)
 
 
 def solve_and_gather_t(full_t, operator_t, n, collective_id):
@@ -359,12 +359,14 @@
     gram_first_part = gram_of(first_factor)
     gram_second_part = gram_of(second_factor)
     block_t = col_gather_t(first_factor.T, n)
-    frame_part = frame_pass(tensor, block_t, second_values.T).T
+    frame_part_t = frame_pass(tensor, block_t, second_values.T)
     scaled_second = gram_second_part * (1.0 / lax.axis_size("row"))
-    summed = all_reduce(jnp.concatenate([frame_part, gram_first_part, scaled_second], axis=1), n, 3)
-    frame_sum = summed[:, :frame_count]
-    gram_first = summed[:, frame_count:frame_count + components]
-    gram_second = summed[:, frame_count + components:]
+    summed_t = all_reduce_t(
+        jnp.concatenate([frame_part_t, gram_first_part.T, scaled_second.T], axis=0), n, 3
+    )
+    frame_sum = summed_t[:frame_count].T
+    gram_first = summed_t[frame_count:frame_count + components].T
+    gram_second = summed_t[frame_count + components:].T
     frames = ridge_solve(gram_first * gram_second, frame_sum)
     gram_frames = jnp.dot(frames, frames.T, precision=lax.Precision.HIGHEST)
     full_part = accumulate_pass_t(tensor, frames, second_values)

time: 185 us -> 186 us (level)
  no operation moved by 1% of the time
where the time goes in v11:
time: 186 us; the launch traced here: 185 us
  Pallas kernels  131 us (70%)
  other arithmetic  41.2 us (22%)
  local copies, waits for them, and re-layouts  8.16 us (4%)
  matrix products  3.41 us (2%)
    pallas_call x5, Pallas kernels, col_exchange(): pl.pallas_call(functools.partial(_exchange_kernel, n, rows, mode), out_sh...  101 us
    another operation x9, other arithmetic, ridge_solve(): jnp.linalg.cholesky(gram + ridge_weight * jnp.eye(order_size, dtype=jnp.f...  19.6 us
    another operation x6, other arithmetic, ridge_solve(): lax.linalg.triangular_solve(factor_low, middle, left_side=True, lower=Tru...  16.6 us
    pallas_call x2, Pallas kernels, accumulate_pass_t(): pl.pallas_call(_accumulate_kernel, grid=(frame_count // STREAM_FRAMES,),...  16.5 us
    pallas_call x1, Pallas kernels, second_pass(): pl.pallas_call(_second_kernel, grid=(frame_count // PROJECT_FRAMES,), in_...  7.12 us
    pallas_call x1, Pallas kernels, frame_pass(): pl.pallas_call(_frame_kernel, grid=(frame_count // PROJECT_FRAMES,), in_s...  7.11 us

profile of v11, /device:TPU:24, one launch (start us, length us, event | category | flops | bytes accessed | tf_op | source)
XLA Modules:
  0.0 185.0 jit_solution(12462967677102510509)
XLA Ops:
  0.7 20.4 %shard_map.50 = bf16[8,8,16,64]{3,2,1,0:T(8,128)(2,1)} custom-call(bf16[16,64]{1,0:T(8,128)(2,1)} %bitcast.78), custom_call_target="tpu_custom_call" | custom-call | tf_op jit(solution)/shard_map/pallas_call | solution.py:304
  21.1 1.3 convert_bitcast_fusion.second_t_ref
  22.4 7.1 %shard_map.51 = f32[128,64]{1,0:T(8,128)} custom-call(bf16[1024,64]{1,0:T(8,128)(2,1)} %bitcast.72, f32[48,64]{1,0:T(8,128)} %convert_bitcast_fusion.second_t_ref, bf16[128,48,1024]{2,1,0:T(8,128)(2,1)} %slab_ref.7), custom_call_target="tpu_custom_call" | custom-call | flops 805306368 | bytes 12582912 | tf_op jit(solution)/shard_map/pallas_call | solution.py:65
  29.9 1.5 pad_maximum_fusion
  31.4 24.3 %shard_map.52 = f32[8,8,4,64]{3,2,1,0:T(4,128)} custom-call(f32[8,8,4,64]{3,2,1,0:T(4,128)} %bitcast.73), custom_call_target="tpu_custom_call" | custom-call | tf_op jit(solution)/shard_map/pallas_call | solution.py:304
  56.8 5.9 %cholesky.59 = f32[64,64]{1,0:T(8,128)S(1)} custom-call(f32[64,64]{1,0:T(8,128)S(1)} %copy.24), custom_call_target="Cholesky" | custom-call | tf_op jit(solution)/shard_map/jit(cholesky)/cholesky | solution.py:16
  64.0 4.9 %custom-call.17 = f32[1,64,64]{1,2,0:T(8,128)S(1)} custom-call(f32[1,64,64]{2,1,0:T(8,128)S(1)} %fusion), custom_call_target="InvertDiagBlocksLowerTriangular" | custom-call | tf_op jit(solution)/shard_map/triangular_solve | solution.py:18
  68.9 0.9 slice.56
  70.6 5.9 %cholesky.70 = f32[64,64]{1,0:T(8,128)S(1)} custom-call(f32[64,64]{1,0:T(8,128)S(1)} %copy.27), custom_call_target="Cholesky" | custom-call | tf_op jit(solution)/shard_map/jit(cholesky)/cholesky | solution.py:16
  77.8 4.9 %custom-call.18 = f32[1,64,64]{1,2,0:T(8,128)S(1)} custom-call(f32[1,64,64]{2,1,0:T(8,128)S(1)} %fusion.1), custom_call_target="InvertDiagBlocksLowerTriangular" | custom-call | tf_op jit(solution)/shard_map/triangular_solve | solution.py:18
  83.9 1.4 tile.9.tiled_ref
  85.3 8.3 %shard_map.53 = f32[1024,64]{1,0:T(8,128)} custom-call(f32[64,128]{1,0:T(8,128)} %copy-done, f32[64,1536]{1,0:T(8,128)} %tile.9.tiled_ref, bf16[128,48,1024]{2,1,0:T(8,128)(2,1)} %slab_ref.7), custom_call_target="tpu_custom_call" | custom-call | flops 805306368 | bytes 12582912 | tf_op jit(solution)/shard_map/pallas_call | solution.py:133
  93.6 29.0 %shard_map.54 = bf16[8,8,16,64]{3,2,1,0:T(8,128)(2,1)} custom-call(f32[8,8,16,64]{3,2,1,0:T(8,128)} %bitcast.69, f32[64,64]{1,0:T(8,128)} %fusion.8.refs_1_), custom_call_target="tpu_custom_call" | custom-call | tf_op jit(solution)/shard_map/pallas_call | solution.py:304
  122.6 1.5 copy.28
  124.2 7.1 %shard_map.55 = f32[48,64]{1,0:T(8,128)} custom-call(bf16[1024,64]{1,0:T(8,128)(2,1)} %bitcast.71, f32[128,64]{1,0:T(8,128)} %bitcast.74, bf16[128,48,1024]{2,1,0:T(8,128)(2,1)} %slab_ref.7), custom_call_target="tpu_custom_call" | custom-call | flops 805306368 | bytes 12582912 | tf_op jit(solution)/shard_map/pallas_call | solution.py:83
  131.5 1.4 pad_maximum_fusion.1.refs_0_
  132.9 6.3 %shard_map.56 = f32[112,64]{1,0:T(8,128)} custom-call(f32[112,64]{1,0:T(8,128)} %pad_maximum_fusion.1.refs_0_), custom_call_target="tpu_custom_call" | custom-call | tf_op jit(solution)/shard_map/pallas_call | solution.py:304
  140.1 5.9 %cholesky.81 = f32[64,64]{1,0:T(8,128)S(1)} custom-call(f32[64,64]{1,0:T(8,128)S(1)} %copy.31), custom_call_target="Cholesky" | custom-call | tf_op jit(solution)/shard_map/jit(cholesky)/cholesky | solution.py:16
  147.3 4.9 %custom-call.19 = f32[1,64,64]{1,2,0:T(8,128)S(1)} custom-call(f32[1,64,64]{2,1,0:T(8,128)S(1)} %fusion.2), custom_call_target="InvertDiagBlocksLowerTriangular" | custom-call | tf_op jit(solution)/shard_map/triangular_solve | solution.py:18
  152.2 1.0 fusion.5
  153.4 1.4 tile.21.tiled_ref
  154.8 8.3 %shard_map.57 = f32[1024,64]{1,0:T(8,128)} custom-call(f32[64,128]{1,0:T(8,128)} %copy-done, f32[64,1536]{1,0:T(8,128)} %tile.21.tiled_ref, bf16[128,48,1024]{2,1,0:T(8,128)(2,1)} %slab_ref.7), custom_call_target="tpu_custom_call" | custom-call | flops 805306368 | bytes 12582912 | tf_op jit(solution)/shard_map/pallas_call | solution.py:133
  163.1 20.6 %shard_map.58 = f32[16,64]{1,0:T(8,128)} custom-call(f32[8,8,16,64]{3,2,1,0:T(8,128)} %bitcast.70), custom_call_target="tpu_custom_call" | custom-call | tf_op jit(solution)/shard_map/pallas_call | solution.py:304
  183.7 1.3 copy.39
  (43 shorter events, 8.8 us)
Async XLA Ops:
  0.6 29.1 %copy-start.3 = (bf16[64,16]{0,1:T(8,128)(2,1)S(1)}, bf16[64,16]{0,1:T(8,128)(2,1)}, u32[]{:S(2)}) copy-start(bf16[64,16]{0,1:T(8,128)(2,1)} %param.5) | copy-start | bytes 6148
  0.6 28.9 %copy-start.2 = (bf16[64,48]{0,1:T(8,128)(2,1)S(1)}, bf16[64,48]{0,1:T(8,128)(2,1)}, u32[]{:S(2)}) copy-start(bf16[64,48]{0,1:T(8,128)(2,1)} %param.6) | copy-start | bytes 18436
  70.2 15.1 %copy-start = (f32[64,128]{1,0:T(8,128)}, f32[64,128]{1,0:T(8,128)S(1)}, u32[]{:S(2)}) copy-start(f32[64,128]{1,0:T(8,128)S(1)} %fusion.13.frames_ref) | copy-start | bytes 98308
  122.6 8.7 %copy-start.1 = (bf16[8,8,16,64]{3,2,1,0:T(8,128)(2,1)S(1)}, bf16[8,8,16,64]{3,2,1,0:T(8,128)(2,1)}, u32[]{:S(2)}) copy-start(bf16[8,8,16,64]{3,2,1,0:T(8,128)(2,1)} %shard_map.54) | copy-start | bytes 393220

commit v12 on v9

--- a/solution.py
+++ b/solution.py
@@ -1,6 +1,7 @@
 import functools
 
 import jax
+import numpy as np
 import jax.numpy as jnp
 from jax import lax
 from jax.experimental import pallas as pl
@@ -97,7 +98,7 @@
     )(block_t, frames_t, tensor)
 
 
-def _accumulate_kernel(frames_ref, tiled_ref, slab_ref, out_ref, total_ref):
+def _accumulate_kernel(frames_ref, tiled_ref, expand_ref, slab_ref, out_ref, total_ref):
     frames, width, rows = slab_ref.shape
     step = pl.program_id(0)
 
@@ -105,11 +106,8 @@
     def _():
         total_ref[...] = jnp.zeros_like(total_ref)
 
-    frame_count = frames_ref.shape[1]
     span = frames * width
-    which = lax.broadcasted_iota(jnp.int32, (frame_count, span), 0) - step * frames
-    column = lax.broadcasted_iota(jnp.int32, (frame_count, span), 1)
-    expand = ((column >= which * width) & (column < which * width + width)).astype(jnp.bfloat16)
+    expand = expand_ref[...]
     rest = frames_ref[...]
     repeated = jnp.zeros((frames_ref.shape[0], span), jnp.float32)
     for _ in range(3):
@@ -130,10 +128,22 @@
     frame_count, width, rows = tensor.shape
     components = frames.shape[0]
     tiled = jnp.tile(second, (1, STREAM_FRAMES))
+    steps = frame_count // STREAM_FRAMES
+    span = STREAM_FRAMES * width
+    owner = np.arange(frame_count)[:, None] - np.arange(steps)[:, None, None] * STREAM_FRAMES
+    column = np.arange(span)[None, None, :]
+    expand = jnp.asarray(
+        ((column >= owner * width) & (column < owner * width + width)).astype(np.float32),
+        jnp.bfloat16,
+    )
     return pl.pallas_call(
         _accumulate_kernel,
-        grid=(frame_count // STREAM_FRAMES,),
-        in_specs=[_whole(frames.shape), _whole(tiled.shape), _slab_spec(width, rows)],
+        grid=(steps,),
+        in_specs=[
+            _whole(frames.shape), _whole(tiled.shape),
+            pl.BlockSpec((None, frame_count, span), lambda s: (s, 0, 0)),
+            _slab_spec(width, rows),
+        ],
         out_specs=_whole((rows, components)),
         out_shape=jax.ShapeDtypeStruct((rows, components), jnp.float32),
         scratch_shapes=[pltpu.VMEM((components, rows), jnp.float32)],
@@ -141,7 +151,7 @@
             flops=2 * components * frame_count * width * rows, transcendentals=0,
             bytes_accessed=2 * frame_count * width * rows,
         ),
-    )(frames, tiled, tensor)
+    )(frames, tiled, expand, tensor)
 
 
 def _split(n):

time: 185 us -> 185 us (level)
  no operation moved by 1% of the time
where the time goes in v12:
time: 185 us; the launch traced here: 184 us
  Pallas kernels  131 us (71%)
  other arithmetic  41.4 us (22%)
  local copies, waits for them, and re-layouts  7.34 us (4%)
  matrix products  3.44 us (2%)
    pallas_call x5, Pallas kernels, col_exchange(): pl.pallas_call(functools.partial(_exchange_kernel, n, rows, mode), out_sh...  101 us
    another operation x9, other arithmetic, ridge_solve(): jnp.linalg.cholesky(gram + ridge_weight * jnp.eye(order_size, dtype=jnp.f...  19.6 us
    another operation x6, other arithmetic, ridge_solve(): lax.linalg.triangular_solve(factor_low, middle, left_side=True, lower=Tru...  16.6 us
    pallas_call x2, Pallas kernels, accumulate_pass_t(): pl.pallas_call(_accumulate_kernel, grid=(steps,), in_specs=[_whole(frames...  16.5 us
    pallas_call x1, Pallas kernels, frame_pass(): pl.pallas_call(_frame_kernel, grid=(frame_count // PROJECT_FRAMES,), in_s...  7.11 us
    pallas_call x1, Pallas kernels, second_pass(): pl.pallas_call(_second_kernel, grid=(frame_count // PROJECT_FRAMES,), in_...  7.11 us

profile of v12, /device:TPU:24, one launch (start us, length us, event | category | flops | bytes accessed | tf_op | source)
XLA Modules:
  0.0 184.4 jit_solution(9847852183416816419)
XLA Ops:
  0.7 20.4 %shard_map.68 = bf16[8,8,16,64]{3,2,1,0:T(8,128)(2,1)} custom-call(bf16[16,64]{1,0:T(8,128)(2,1)} %bitcast.74), custom_call_target="tpu_custom_call" | custom-call | tf_op jit(solution)/shard_map/pallas_call | solution.py:314
  21.1 1.3 convert_bitcast_fusion.second_t_ref
  22.4 7.1 %shard_map.69 = f32[128,64]{1,0:T(8,128)} custom-call(bf16[1024,64]{1,0:T(8,128)(2,1)} %bitcast.64, f32[48,64]{1,0:T(8,128)} %convert_bitcast_fusion.second_t_ref, bf16[128,48,1024]{2,1,0:T(8,128)(2,1)} %slab_ref.7), custom_call_target="tpu_custom_call" | custom-call | flops 805306368 | bytes 12582912 | tf_op jit(solution)/shard_map/pallas_call | solution.py:66
  29.9 1.5 pad_maximum_fusion
  31.4 24.3 %shard_map.70 = f32[8,8,4,64]{3,2,1,0:T(4,128)} custom-call(f32[8,8,4,64]{3,2,1,0:T(4,128)} %bitcast.69), custom_call_target="tpu_custom_call" | custom-call | tf_op jit(solution)/shard_map/pallas_call | solution.py:314
  55.7 1.0 copy.22
  57.0 5.9 %cholesky.59 = f32[64,64]{1,0:T(8,128)S(1)} custom-call(f32[64,64]{1,0:T(8,128)S(1)} %copy.24), custom_call_target="Cholesky" | custom-call | tf_op jit(solution)/shard_map/jit(cholesky)/cholesky | solution.py:17
  64.2 4.9 %custom-call.17 = f32[1,64,64]{1,2,0:T(8,128)S(1)} custom-call(f32[1,64,64]{2,1,0:T(8,128)S(1)} %fusion), custom_call_target="InvertDiagBlocksLowerTriangular" | custom-call | tf_op jit(solution)/shard_map/triangular_solve | solution.py:19
  69.9 5.9 %cholesky.70 = f32[64,64]{1,0:T(8,128)S(1)} custom-call(f32[64,64]{1,0:T(8,128)S(1)} %copy.27), custom_call_target="Cholesky" | custom-call | tf_op jit(solution)/shard_map/jit(cholesky)/cholesky | solution.py:17
  77.1 4.9 %custom-call.18 = f32[1,64,64]{1,2,0:T(8,128)S(1)} custom-call(f32[1,64,64]{2,1,0:T(8,128)S(1)} %fusion.1), custom_call_target="InvertDiagBlocksLowerTriangular" | custom-call | tf_op jit(solution)/shard_map/triangular_solve | solution.py:19
  83.2 1.4 tile.9.tiled_ref
  84.7 8.3 %shard_map.71 = f32[1024,64]{1,0:T(8,128)} custom-call(f32[64,128]{1,0:T(8,128)} %copy-done, f32[64,1536]{1,0:T(8,128)} %tile.9.tiled_ref, bf16[4,128,1536]{2,1,0:T(8,128)(2,1)} %constant.58.clone.expand_ref, bf16[128,48,1024]{2,1,0:T(8,128)(2,1)} %slab_ref.7), custom_call_target="tpu_custom_call" | custom-call | flops 805306368 | bytes 12582912 | tf_op jit(solution)/shard_map/pallas_call | solution.py:139
  92.9 29.0 %shard_map.72 = bf16[8,8,16,64]{3,2,1,0:T(8,128)(2,1)} custom-call(f32[8,8,16,64]{3,2,1,0:T(8,128)} %bitcast.61, f32[64,64]{1,0:T(8,128)} %fusion.10.refs_1_), custom_call_target="tpu_custom_call" | custom-call | tf_op jit(solution)/shard_map/pallas_call | solution.py:314
  122.0 1.5 copy.28
  123.5 7.1 %shard_map.73 = f32[48,64]{1,0:T(8,128)} custom-call(bf16[1024,64]{1,0:T(8,128)(2,1)} %bitcast.63, f32[128,64]{1,0:T(8,128)} %bitcast.71, bf16[128,48,1024]{2,1,0:T(8,128)(2,1)} %slab_ref.7), custom_call_target="tpu_custom_call" | custom-call | flops 805306368 | bytes 12582912 | tf_op jit(solution)/shard_map/pallas_call | solution.py:84
  130.9 1.4 pad_maximum_fusion.1.refs_0_
  132.2 6.3 %shard_map.74 = f32[112,64]{1,0:T(8,128)} custom-call(f32[112,64]{1,0:T(8,128)} %pad_maximum_fusion.1.refs_0_), custom_call_target="tpu_custom_call" | custom-call | tf_op jit(solution)/shard_map/pallas_call | solution.py:314
  139.4 5.9 %cholesky.81 = f32[64,64]{1,0:T(8,128)S(1)} custom-call(f32[64,64]{1,0:T(8,128)S(1)} %copy.31), custom_call_target="Cholesky" | custom-call | tf_op jit(solution)/shard_map/jit(cholesky)/cholesky | solution.py:17
  146.6 4.9 %custom-call.19 = f32[1,64,64]{1,2,0:T(8,128)S(1)} custom-call(f32[1,64,64]{2,1,0:T(8,128)S(1)} %fusion.2), custom_call_target="InvertDiagBlocksLowerTriangular" | custom-call | tf_op jit(solution)/shard_map/triangular_solve | solution.py:19
  151.5 1.0 fusion.7
  152.8 1.4 tile.21.tiled_ref
  154.2 8.3 %shard_map.75 = f32[1024,64]{1,0:T(8,128)} custom-call(f32[64,128]{1,0:T(8,128)} %copy-done, f32[64,1536]{1,0:T(8,128)} %tile.21.tiled_ref, bf16[4,128,1536]{2,1,0:T(8,128)(2,1)} %constant.58.clone.expand_ref, bf16[128,48,1024]{2,1,0:T(8,128)(2,1)} %slab_ref.7), custom_call_target="tpu_custom_call" | custom-call | flops 805306368 | bytes 12582912 | tf_op jit(solution)/shard_map/pallas_call | solution.py:139
  162.5 20.6 %shard_map.76 = f32[16,64]{1,0:T(8,128)} custom-call(f32[8,8,16,64]{3,2,1,0:T(8,128)} %bitcast.62), custom_call_target="tpu_custom_call" | custom-call | tf_op jit(solution)/shard_map/pallas_call | solution.py:314
  183.1 1.3 copy.39
  (40 shorter events, 8.1 us)
Async XLA Ops:
  0.6 29.1 %copy-start.3 = (bf16[64,16]{0,1:T(8,128)(2,1)S(1)}, bf16[64,16]{0,1:T(8,128)(2,1)}, u32[]{:S(2)}) copy-start(bf16[64,16]{0,1:T(8,128)(2,1)} %param.7) | copy-start | bytes 6148
  0.6 28.9 %copy-start.2 = (bf16[64,48]{0,1:T(8,128)(2,1)S(1)}, bf16[64,48]{0,1:T(8,128)(2,1)}, u32[]{:S(2)}) copy-start(bf16[64,48]{0,1:T(8,128)(2,1)} %param.8) | copy-start | bytes 18436
  69.5 15.1 %copy-start = (f32[64,128]{1,0:T(8,128)}, f32[64,128]{1,0:T(8,128)S(1)}, u32[]{:S(2)}) copy-start(f32[64,128]{1,0:T(8,128)S(1)} %fusion.15.frames_ref) | copy-start | bytes 98308
  122.0 8.6 %copy-start.1 = (bf16[8,8,16,64]{3,2,1,0:T(8,128)(2,1)S(1)}, bf16[8,8,16,64]{3,2,1,0:T(8,128)(2,1)}, u32[]{:S(2)}) copy-start(bf16[8,8,16,64]{3,2,1,0:T(8,128)(2,1)} %shard_map.72) | copy-start | bytes 393220
